TPU v7x, 256 devices: a whole 4x4x8 slice. The times are simulated.
256 devices in a mesh: section: 4 (over x), blk: 64 (over y, z, core).
Axes of the slice: x: 4, y: 4, z: 8, core: 2. Of those that a mesh axis runs over, the one named last changes fastest.
Arguments:
- inputs: bfloat16 [4096, 8192], P(None, 'blk'), may hold values from -6 to 6
- cotangent: bfloat16 [4096, 8192], P(None, 'blk'), may hold values from -6 to 6
- r_weight: bfloat16 [4, 64, 128, 128], P('section', 'blk'), may hold values from -0.5 to 0.5
- g_weight: bfloat16 [4, 64, 128, 128], P('section', 'blk'), may hold values from -0.5 to 0.5
- l_weight: bfloat16 [4, 128, 64, 64], P('section', 'blk'), may hold values from -0.75 to 0.75
Outputs:
- input_grad: bfloat16 [4, 4096, 8192], P('section', None, 'blk')
- r_grad: float32 [4, 64, 128, 128], P('section', 'blk')
- g_grad: float32 [4, 64, 128, 128], P('section', 'blk')
- l_grad: float32 [4, 128, 64, 64], P('section', 'blk')
All inputs are finite; a program needn't handle non-finite values.
Results may differ from a plain program's by a relative error of at most 0.014.
Values may be sent and summed in bfloat16 or wider, within the bound.
No kernel may reach another device: no remote copies, remote signals or barrier semaphores. Data moves between devices by JAX's collectives and lax.ppermute only.
A program may use at most 192 MiB of HBM per device.

v0:
```python
import jax
import jax.numpy as jnp
from jax import lax
from jax.experimental import pallas as pl
from jax.experimental.pallas import tpu as pltpu
from jax.sharding import Mesh, PartitionSpec as P

BF = jnp.bfloat16
F32 = jnp.float32


def nn(a, b):
    return lax.dot_general(a, b, (((1,), (0,)), ((), ())), preferred_element_type=F32)


def nt(a, b):
    return lax.dot_general(a, b, (((1,), (1,)), ((), ())), preferred_element_type=F32)


def feature_order(rows, cols, transposed=False, offset=0):
    r = lax.broadcasted_iota(jnp.int32, (rows, cols), 1 if transposed else 0)
    c = lax.broadcasted_iota(jnp.int32, (rows, cols), 0 if transposed else 1)
    natural = ((r >> 2) & 1) * 128 + (r >> 3) * 4 + (r & 3)
    return jnp.where(natural == c + offset, 1.0, 0.0).astype(BF)


def position_order(rows, cols, transposed=False):
    r = lax.broadcasted_iota(jnp.int32, (rows, cols), 1 if transposed else 0)
    c = lax.broadcasted_iota(jnp.int32, (rows, cols), 0 if transposed else 1)
    natural = (r & 3) * 64 + (r >> 3) * 2 + ((r >> 2) & 1)
    return jnp.where(natural == c, 1.0, 0.0).astype(BF)


def rows_of(ref):
    d, i, n = ref.shape
    return ref[...].astype(F32).reshape(d * i, n)


def put_rows(ref, value):
    ref[...] = value.reshape(ref.shape).astype(ref.dtype)


def block_of(own_ref, other_ref, c, core, k, start, stop):
    mine = own_ref[k, start:stop, :].astype(F32)
    other = other_ref[k, start:stop, :].astype(F32)
    return jnp.where(core == c, mine, other)


def prepare_kernel(at_ref, *refs):
    shifted, other_ref = refs[:4], refs[4]
    outs, own_ref = refs[5:-1], refs[-1]
    sect, core = at_ref[0], at_ref[1]
    for k in range(4):
        own_ref[k] = shifted[k][...]
    p = feature_order(256, 256)
    q = position_order(256, 256)
    lane = lax.broadcasted_iota(jnp.int32, (64, 128), 1)
    for layer in range(4):
        k = lax.rem(sect - layer + 4, 4)
        r_out, rt_out, g_out, gt_out, l_out, lt_out = outs[6 * layer : 6 * layer + 6]
        for start, plain, flipped in ((0, r_out, rt_out), (128, g_out, gt_out)):
            blocks = [
                block_of(own_ref, other_ref, c, core, k, start, start + 128).astype(BF)
                for c in range(2)
            ]
            parts = [p[:, 128 * c : 128 * c + 128] for c in range(2)]
            left = jnp.concatenate([nn(parts[c], blocks[c]) for c in range(2)], axis=1).astype(BF)
            plain[...] = nt(left, p).astype(BF)
            left = jnp.concatenate([nt(parts[c], blocks[c]) for c in range(2)], axis=1).astype(BF)
            flipped[...] = nt(left, p).astype(BF)
        pairs = []
        for c in range(2):
            packed = block_of(own_ref, other_ref, c, core, k, 256, 320)
            low = jnp.where(lane < 64, packed, 0.0)
            high = jnp.where(lane < 64, 0.0, packed)
            pairs.append(jnp.concatenate([low, high], axis=0).astype(BF))
        parts = [q[:, 128 * c : 128 * c + 128] for c in range(2)]
        left = jnp.concatenate([nn(parts[c], pairs[c]) for c in range(2)], axis=1).astype(BF)
        l_out[...] = nt(left, q).astype(BF)
        left = jnp.concatenate([nt(parts[c], pairs[c]) for c in range(2)], axis=1).astype(BF)
        lt_out[...] = nt(left, q).astype(BF)


def turned(core, mine_ref, other_ref):
    p = feature_order(256, 128, offset=core * 128)
    o = feature_order(256, 128, offset=128 - core * 128)
    return (nt(p, mine_ref[...]) + nt(o, other_ref[...])).astype(BF)


def turn_kernel(at_ref, mine_ref, other_ref, o_ref):
    o_ref[...] = turned(at_ref[1], mine_ref, other_ref)


def first_kernel(at_ref, mine_ref, other_ref, rt_ref, x_ref, z_ref):
    x = turned(at_ref[1], mine_ref, other_ref)
    x_ref[...] = x
    put_rows(z_ref, nn(rt_ref[...], x))


def mix_kernel(z_ref, w_ref, u_ref):
    put_rows(u_ref, nn(w_ref[...], rows_of(z_ref).astype(BF)))


def gated_kernel(x_ref, u_ref, gt_ref, rt_ref, x_out, z_ref):
    x = x_ref[...]
    sig = jax.nn.sigmoid(nn(gt_ref[...], x))
    new = (x.astype(F32) + rows_of(u_ref) * sig).astype(BF)
    x_out[...] = new
    put_rows(z_ref, nn(rt_ref[...], new))


def gate_back(upper, x, u, gt, gu_ref, gg_ref):
    sig = jax.nn.sigmoid(nn(gt, x))
    put_rows(gu_ref, upper * sig)
    gg_ref[...] = (upper * u * sig * (1.0 - sig)).astype(BF)


def back_start_kernel(y_ref, x_ref, u_ref, gt_ref, gu_ref, gg_ref):
    gate_back(y_ref[...].astype(F32), x_ref[...], rows_of(u_ref), gt_ref[...], gu_ref, gg_ref)


def lower_of(y_ref, gz_ref, gg_ref, r_ref, g_ref):
    gz = rows_of(gz_ref).astype(BF)
    lower = y_ref[...].astype(F32) + nn(r_ref[...], gz)
    return (lower + nn(g_ref[...], gg_ref[...])).astype(BF)


def back_kernel(y_ref, gz_ref, gg_ref, r_ref, g_ref, x_ref, u_ref, gt_ref, y_out, gu_ref, gg_out):
    lower = lower_of(y_ref, gz_ref, gg_ref, r_ref, g_ref)
    y_out[...] = lower
    gate_back(lower.astype(F32), x_ref[...], rows_of(u_ref), gt_ref[...], gu_ref, gg_out)


def parts_of(x, gz, gg, z, gu, y):
    pt = feature_order(256, 256, True)
    qt = position_order(256, 256, True)
    x_n = nn(pt, x).astype(BF)
    gz_n = nn(pt, gz).astype(BF)
    gg_n = nn(pt, gg).astype(BF)
    z_n = nn(qt, z).astype(BF)
    gu_n = nn(qt, gu).astype(BF)
    y_n = nn(pt, y)
    lane = lax.broadcasted_iota(jnp.int32, (64, 128), 1)
    parts = []
    for i in range(2):
        at = slice(128 * i, 128 * i + 128)
        l_part = nt(z_n[at], gu_n[at])
        parts.append(
            (
                y_n[at].T,
                nt(x_n[at], gz_n[at]),
                nt(x_n[at], gg_n[at]),
                jnp.where(lane < 64, l_part[:64], l_part[64:]),
            )
        )
    return parts


def put_parts(core, parts, mine_out, other_out):
    start = 0
    for low, high in zip(*parts):
        stop = start + low.shape[0]
        mine_out[start:stop, :] = jnp.where(core == 0, low, high).astype(BF)
        other_out[start:stop, :] = jnp.where(core == 0, high, low).astype(BF)
        start = stop


def parts_kernel(at_ref, x_ref, gz_ref, gg_ref, z_ref, gu_ref, y_ref, mine_out, other_out):
    parts = parts_of(
        x_ref[...],
        rows_of(gz_ref).astype(BF),
        gg_ref[...],
        rows_of(z_ref).astype(BF),
        rows_of(gu_ref).astype(BF),
        y_ref[...],
    )
    put_parts(at_ref[1], parts, mine_out, other_out)


def last_kernel(
    at_ref, x_ref, gz_ref, gg_ref, z_ref, gu_ref, y_ref, r_ref, g_ref, mine_out, other_out
):
    lower = lower_of(y_ref, gz_ref, gg_ref, r_ref, g_ref)
    parts = parts_of(
        x_ref[...],
        rows_of(gz_ref).astype(BF),
        gg_ref[...],
        rows_of(z_ref).astype(BF),
        rows_of(gu_ref).astype(BF),
        lower,
    )
    put_parts(at_ref[1], parts, mine_out, other_out)


def join(core, mine_ref, other_ref, out_ref):
    n = (out_ref.shape[0] - 320) // 2
    out_ref[pl.ds(pl.multiple_of(core * n, n), n), :] = mine_ref[:n, :]
    out_ref[pl.ds(pl.multiple_of((1 - core) * n, n), n), :] = other_ref[:n, :]
    total = mine_ref[n:, :].astype(F32) + other_ref[n:, :].astype(F32)
    out_ref[2 * n :, :] = total.astype(BF)


def join_kernel(at_ref, mine_ref, other_ref, out_ref):
    join(at_ref[1], mine_ref, other_ref, out_ref)


def route_kernel(at_ref, *refs):
    sect, core = at_ref[0], at_ref[1]
    mine, other, outs = refs[:3], refs[3:6], refs[6:]
    for k in range(4):
        target = lax.rem(sect + k, 4)

        @pl.when(target == 0)
        def _():
            outs[k][...] = jnp.zeros_like(outs[k])

        for layer in range(1, 4):

            @pl.when(target == layer)
            def _():
                join(core, mine[layer - 1], other[layer - 1], outs[k])


def settle_kernel(at_ref, *refs):
    early, late = refs[:4], refs[4:8]
    y_out, r_out, g_out, l_out = refs[8:]
    sect = at_ref[0]
    n = y_out.shape[0] // 4

    def settle(parts):
        total = None
        for k in range(4):
            source = pl.multiple_of(lax.rem(sect - k + 4, 4) * n, n)
            y_out[pl.ds(source, n), :] = parts[k][:n, :]
            part = parts[k][n:, :].astype(F32)
            total = part if total is None else total + part
        r_out[...] = total[:128]
        g_out[...] = total[128:256]
        l_out[0] = total[256:, :64]
        l_out[1] = total[256:, 64:]

    @pl.when(sect == 0)
    def _():
        settle(late)

    @pl.when(sect != 0)
    def _():
        settle(early)


def run(kernel, outs, *args, dots=1, at=None, scratch=(), blocks=None):
    nbytes = sum(a.size * a.dtype.itemsize for a in args)
    params = pltpu.CompilerParams(vmem_limit_bytes=16 << 20)
    cost = pl.CostEstimate(
        flops=dots * 2 * 256 * 256 * 512, bytes_accessed=2 * nbytes, transcendentals=0
    )
    if at is None:
        return pl.pallas_call(
            kernel, out_shape=outs, compiler_params=params, cost_estimate=cost
        )(*args)
    specs = [
        spec or pl.BlockSpec(a.shape, lambda i, at, nd=a.ndim: (0,) * nd)
        for a, spec in zip(args, blocks or [None] * len(args))
    ]
    many = isinstance(outs, list)
    out_specs = [
        pl.BlockSpec(o.shape, lambda i, at, nd=len(o.shape): (0,) * nd)
        for o in (outs if many else [outs])
    ]
    return pl.pallas_call(
        kernel,
        out_shape=outs,
        grid_spec=pltpu.PrefetchScalarGridSpec(
            num_scalar_prefetch=1,
            grid=(1,),
            in_specs=specs,
            out_specs=out_specs if many else out_specs[0],
            scratch_shapes=list(scratch),
        ),
        compiler_params=params,
        cost_estimate=cost,
    )(at, *args)


def sds(*shape, dtype=BF):
    return jax.ShapeDtypeStruct(shape, dtype)


def program(inputs, cotangent, r_weight, g_weight, l_weight):
    sections = lax.axis_size("x")
    tokens = inputs.shape[0] // (sections * 2)
    sect = lax.axis_index("x")
    core = lax.axis_index("c")
    at = jnp.stack([sect, core, sect * 2 + core]).astype(jnp.int32)

    def to_other(value):
        return lax.ppermute(value, "c", [(0, 1), (1, 0)])

    def shift(value, k, targets=range(4)):
        route = [(i, (i + k) % sections) for i in range(sections)]
        return lax.ppermute(value, "x", [(i, j) for i, j in route if j in targets])

    l_flat = jnp.concatenate([l_weight[0, 0], l_weight[0, 1]], axis=1)
    packed = jnp.concatenate([r_weight[0, 0], g_weight[0, 0], l_flat], axis=0)
    own = [packed]
    for k in range(1, sections):
        own.append(shift(packed, k))
    other = to_other(jnp.stack(own))

    def sent_over(whole):
        start = (sect * 2 + 1 - core) * tokens
        return to_other(lax.dynamic_slice_in_dim(whole, start, tokens, 0))

    def swap(block):
        return lax.all_to_all(block, ("y", "z"), 0, 0, tiled=True)

    flat = sds(256, tokens)
    sent = sds(32, 8, tokens)
    mine = pl.BlockSpec((tokens, 128), lambda i, at: (at[2], 0))
    outs = run(
        prepare_kernel,
        [sds(256, 256)] * 24,
        *own,
        other,
        at=at,
        dots=24,
        scratch=[pltpu.VMEM((4, 320, 128), BF)],
    )
    mats = [outs[6 * s : 6 * s + 6] for s in range(sections)]
    x0, z = run(
        first_kernel,
        [flat, sent],
        inputs,
        sent_over(inputs),
        mats[0][1],
        at=at,
        dots=2,
        blocks=[mine, None, None],
    )
    crossed = sent_over(cotangent)
    y = run(turn_kernel, flat, cotangent, crossed, at=at, blocks=[mine, None])
    z, y = lax.optimization_barrier((z, y))
    x = [x0]
    z_all, u_all = [], []
    for s in range(sections):
        z = swap(z)
        z_all.append(z)
        u = swap(run(mix_kernel, sent, z, mats[s][5]))
        u_all.append(u)
        if s + 1 < sections:
            new, z = run(gated_kernel, [flat, sent], x[s], u, mats[s][3], mats[s + 1][1], dots=2)
            x.append(new)
    last = sections - 1
    gu, gg = run(back_start_kernel, [sent, flat], y, x[last], u_all[last], mats[last][3])
    rows = sds(tokens + 320, 128)
    joined = sds(2 * tokens + 320, 128)
    kept, crossed = [], []
    for s in range(last, -1, -1):
        gu = swap(gu)
        if s == 0:
            gu, kept, crossed = lax.optimization_barrier((gu, kept, crossed))
        mixed = run(mix_kernel, sent, gu, mats[s][4])
        if s == 0:
            routed = run(route_kernel, [joined] * 4, *kept, *crossed, at=at)
            mixed, routed = lax.optimization_barrier((mixed, routed))
        gz = swap(mixed)
        held = (x[s], gz, gg, z_all[s], gu)
        if s > 0:
            y, gu, gg = run(
                back_kernel,
                [flat, sent, flat],
                y,
                gz,
                gg,
                mats[s][0],
                mats[s][2],
                x[s - 1],
                u_all[s - 1],
                mats[s - 1][3],
                dots=3,
            )
            part, away = run(parts_kernel, [rows, rows], *held, y, at=at, dots=9)
            kept.insert(0, part)
            crossed.insert(0, to_other(away))
    early = [routed[0]]
    for k in range(1, sections):
        early.append(shift(routed[k], k, (1, 2, 3)))
    part, away = run(
        last_kernel, [rows, rows], *held, y, mats[0][0], mats[0][2], at=at, dots=11
    )
    final = run(join_kernel, joined, part, to_other(away), at=at)
    late = [final] + [shift(final, k, (0,)) for k in range(1, sections)]
    y_out, r_grad, g_grad, l_grad = run(
        settle_kernel,
        [
            sds(sections * 2 * tokens, 128),
            sds(128, 128, dtype=F32),
            sds(128, 128, dtype=F32),
            sds(2, 64, 64, dtype=F32),
        ],
        *early,
        *late,
        at=at,
    )
    return y_out[None], r_grad[None, None], g_grad[None, None], l_grad[None]


def solution(mesh):
    grid = Mesh(mesh.devices.reshape(4, 4, 8, 2), ("x", "y", "z", "c"))
    blk = ("y", "z", "c")
    return jax.shard_map(
        program,
        mesh=grid,
        in_specs=(
            P(None, blk),
            P(None, blk),
            P("x", blk, None, None),
            P("x", blk, None, None),
            P("x", blk, None, None),
        ),
        out_specs=(
            P("x", None, blk),
            P("x", blk, None, None),
            P("x", blk, None, None),
            P("x", blk, None, None),
        ),
        check_vma=False,
    )
```

profile of v0, /device:TPU:1, one launch (start us, length us, event | category | flops | bytes accessed | tf_op | source)
XLA Modules:
  0.0 330.3 jit_solution(17118141298925585251)
XLA Ops:
  0.7 0.8 slice_bitcast_fusion.1
  1.6 3.3 %collective-permute-start.3 = (bf16[320,128]{1,0:T(8,128)(2,1)S(1)}, bf16[320,128]{1,0:T(8,128)(2,1)S(1)}, u32[]{:S(2)}, u32[]{:S(2)}) collective-permute-start(bf16[320,128]{1,0:T(8,128)(2,1)S(1)} %maximum_maximum_fusion.refs_0_), channel_id=1, source_target_pairs={{0,192},{64,0},{128,64},{192,128},{1,193},{65,1},{129,65},{193,129... | collective-permute-start | bytes 245768 | tf_op jit(solution)/shard_map/ppermute | solution.py:301
  4.9 0.5 collective-permute-start.2
  5.4 0.6 collective-permute-start.1
  6.4 3.4 %collective-permute-done.2.refs_2_ = bf16[320,128]{1,0:T(8,128)(2,1)S(1)} collective-permute-done((bf16[320,128]{1,0:T(8,128)(2,1)S(1)}, bf16[320,128]{1,0:T(8,128)(2,1)S(1)}, u32[]{:S(2)}, u32[]{:S(2)}) %collective-permute-start.2) | collective-permute-done | bytes 81952 | tf_op jit(solution)/shard_map/ppermute | solution.py:301
  9.8 2.1 collective-permute-done.1.refs_1_
  11.9 1.3 collective-permute-start.4
  13.3 0.9 constant_dynamic-slice_fusion.1
  14.2 0.6 collective-permute-start
  14.8 0.8 shard_map.86.y_ref
  15.7 2.5 shard_map.84
  18.3 1.0 shard_map.85
  19.3 21.1 %all_to_all.80.z_ref = bf16[32,8,512]{2,1,0:T(8,128)(2,1)S(1)} all-to-all(bf16[32,8,512]{2,1,0:T(8,128)(2,1)S(1)} %get-tuple-element.81), channel_id=1, replica_groups=mesh['x'=4,'y'=4,'z'=8,'c'=2] {'y','z'}, dimensions={0} | all-to-all | bytes 524288 | tf_op jit(solution)/shard_map/all_to_all | solution.py:315
  40.7 16.0 %all_to_all.81.u_ref = bf16[32,8,512]{2,1,0:T(8,128)(2,1)S(1)} all-to-all(bf16[32,8,512]{2,1,0:T(8,128)(2,1)S(1)} %shard_map.87), channel_id=1, replica_groups=mesh['x'=4,'y'=4,'z'=8,'c'=2] {'y','z'}, dimensions={0} | all-to-all | bytes 524288 | tf_op jit(solution)/shard_map/all_to_all | solution.py:315
  56.7 0.5 shard_map.88
  57.2 15.6 %all_to_all.82.z_ref = bf16[32,8,512]{2,1,0:T(8,128)(2,1)S(1)} all-to-all(bf16[32,8,512]{2,1,0:T(8,128)(2,1)S(1)} %get-tuple-element.86), channel_id=1, replica_groups=mesh['x'=4,'y'=4,'z'=8,'c'=2] {'y','z'}, dimensions={0} | all-to-all | bytes 524288 | tf_op jit(solution)/shard_map/all_to_all | solution.py:315
  73.0 14.8 %all_to_all.83.u_ref = bf16[32,8,512]{2,1,0:T(8,128)(2,1)S(1)} all-to-all(bf16[32,8,512]{2,1,0:T(8,128)(2,1)S(1)} %shard_map.89), channel_id=1, replica_groups=mesh['x'=4,'y'=4,'z'=8,'c'=2] {'y','z'}, dimensions={0} | all-to-all | bytes 524288 | tf_op jit(solution)/shard_map/all_to_all | solution.py:315
  87.8 0.5 shard_map.90
  88.3 14.1 %all_to_all.84.z_ref = bf16[32,8,512]{2,1,0:T(8,128)(2,1)S(1)} all-to-all(bf16[32,8,512]{2,1,0:T(8,128)(2,1)S(1)} %get-tuple-element.91), channel_id=1, replica_groups=mesh['x'=4,'y'=4,'z'=8,'c'=2] {'y','z'}, dimensions={0} | all-to-all | bytes 524288 | tf_op jit(solution)/shard_map/all_to_all | solution.py:315
  102.7 14.2 %all_to_all.85.u_ref = bf16[32,8,512]{2,1,0:T(8,128)(2,1)S(1)} all-to-all(bf16[32,8,512]{2,1,0:T(8,128)(2,1)S(1)} %shard_map.91), channel_id=1, replica_groups=mesh['x'=4,'y'=4,'z'=8,'c'=2] {'y','z'}, dimensions={0} | all-to-all | bytes 524288 | tf_op jit(solution)/shard_map/all_to_all | solution.py:315
  116.8 0.5 shard_map.92
  117.3 13.9 %all_to_all.86.z_ref = bf16[32,8,512]{2,1,0:T(8,128)(2,1)S(1)} all-to-all(bf16[32,8,512]{2,1,0:T(8,128)(2,1)S(1)} %get-tuple-element.96), channel_id=1, replica_groups=mesh['x'=4,'y'=4,'z'=8,'c'=2] {'y','z'}, dimensions={0} | all-to-all | bytes 524288 | tf_op jit(solution)/shard_map/all_to_all | solution.py:315
  131.4 13.8 %all_to_all.87.u_ref = bf16[32,8,512]{2,1,0:T(8,128)(2,1)S(1)} all-to-all(bf16[32,8,512]{2,1,0:T(8,128)(2,1)S(1)} %shard_map.93), channel_id=1, replica_groups=mesh['x'=4,'y'=4,'z'=8,'c'=2] {'y','z'}, dimensions={0} | all-to-all | bytes 524288 | tf_op jit(solution)/shard_map/all_to_all | solution.py:315
  145.6 13.8 %all_to_all.88.z_ref.gu_ref = bf16[32,8,512]{2,1,0:T(8,128)(2,1)S(1)} all-to-all(bf16[32,8,512]{2,1,0:T(8,128)(2,1)S(1)} %get-tuple-element.99), channel_id=1, replica_groups=mesh['x'=4,'y'=4,'z'=8,'c'=2] {'y','z'}, dimensions={0} | all-to-all | bytes 524288 | tf_op jit(solution)/shard_map/all_to_all | solution.py:315
  159.6 13.9 %all_to_all.89.gz_ref = bf16[32,8,512]{2,1,0:T(8,128)(2,1)S(1)} all-to-all(bf16[32,8,512]{2,1,0:T(8,128)(2,1)S(1)} %shard_map.95), channel_id=1, replica_groups=mesh['x'=4,'y'=4,'z'=8,'c'=2] {'y','z'}, dimensions={0} | all-to-all | bytes 524288 | tf_op jit(solution)/shard_map/all_to_all | solution.py:315
  173.6 0.5 shard_map.96
  174.1 14.4 %all_to_all.90.z_ref.gu_ref = bf16[32,8,512]{2,1,0:T(8,128)(2,1)S(1)} all-to-all(bf16[32,8,512]{2,1,0:T(8,128)(2,1)S(1)} %get-tuple-element.105), channel_id=1, replica_groups=mesh['x'=4,'y'=4,'z'=8,'c'=2] {'y','z'}, dimensions={0} | all-to-all | bytes 524288 | tf_op jit(solution)/shard_map/all_to_all | solution.py:315
  188.8 14.8 %all_to_all.91.gz_ref = bf16[32,8,512]{2,1,0:T(8,128)(2,1)S(1)} all-to-all(bf16[32,8,512]{2,1,0:T(8,128)(2,1)S(1)} %shard_map.97), channel_id=1, replica_groups=mesh['x'=4,'y'=4,'z'=8,'c'=2] {'y','z'}, dimensions={0} | all-to-all | bytes 524288 | tf_op jit(solution)/shard_map/all_to_all | solution.py:315
  203.5 0.5 shard_map.98
  204.0 15.5 %all_to_all.92.z_ref.gu_ref = bf16[32,8,512]{2,1,0:T(8,128)(2,1)S(1)} all-to-all(bf16[32,8,512]{2,1,0:T(8,128)(2,1)S(1)} %get-tuple-element.111), channel_id=1, replica_groups=mesh['x'=4,'y'=4,'z'=8,'c'=2] {'y','z'}, dimensions={0} | all-to-all | bytes 524288 | tf_op jit(solution)/shard_map/all_to_all | solution.py:315
  219.8 15.0 %all_to_all.93.gz_ref = bf16[32,8,512]{2,1,0:T(8,128)(2,1)S(1)} all-to-all(bf16[32,8,512]{2,1,0:T(8,128)(2,1)S(1)} %shard_map.99), channel_id=1, replica_groups=mesh['x'=4,'y'=4,'z'=8,'c'=2] {'y','z'}, dimensions={0} | all-to-all | bytes 524288 | tf_op jit(solution)/shard_map/all_to_all | solution.py:315
  234.8 0.5 shard_map.100
  235.5 0.7 copy-done.6
  236.2 0.7 copy-done.23
  236.9 0.7 copy-done.26
  237.6 6.2 %all-to-all-start.14 = ((bf16[32,8,512]{2,1,0:T(8,128)(2,1)}), bf16[32,8,512]{2,1,0:T(8,128)(2,1)S(1)}, u32[]{:S(2)}, u32[]{:S(2)}) async-start(bf16[32,8,512]{2,1,0:T(8,128)(2,1)} %copy-done.6), calls=%async_computation.14 | async-start | bytes 524288 | tf_op jit(solution)/shard_map/all_to_all | solution.py:315
  243.8 0.9 copy-done.5
  244.8 0.9 copy-done.8
  245.7 0.9 copy-done.14
  246.7 1.3 shard_map.103
  248.1 20.1 %collective-permute-start.8 = (bf16[832,128]{1,0:T(8,128)(2,1)S(1)}, bf16[832,128]{1,0:T(8,128)(2,1)S(1)}, u32[]{:S(2)}, u32[]{:S(2)}) collective-permute-start(bf16[832,128]{1,0:T(8,128)(2,1)S(1)} %get-tuple-element.123), channel_id=1, source_target_pairs={{0,1},{1,0},{2,3},{3,2},{4,5},{5,4},{6,7},{7,6},{8,9},{9,8},{10,11... | collective-permute-start | bytes 638984 | tf_op jit(solution)/shard_map/ppermute | solution.py:297
  268.1 1.3 shard_map.102
  269.6 1.3 shard_map.101
  271.0 0.6 collective-permute-start.6
  271.5 0.7 copy-done.19
  272.6 0.9 shard_map.104
  273.9 1.5 shard_map.105
  275.4 9.6 %all-to-all-start.15 = ((bf16[32,8,512]{2,1,0:T(8,128)(2,1)}), bf16[32,8,512]{2,1,0:T(8,128)(2,1)S(1)}, u32[]{:S(2)}, u32[]{:S(2)}) async-start(bf16[32,8,512]{2,1,0:T(8,128)(2,1)} %shard_map.104), calls=%async_computation.15 | async-start | bytes 524288 | tf_op jit(solution)/shard_map/all_to_all | solution.py:315
  285.0 1.3 collective-permute-start.9
  286.3 8.4 %all-to-all-done.15.gz_ref = bf16[32,8,512]{2,1,0:T(8,128)(2,1)S(1)} async-done(((bf16[32,8,512]{2,1,0:T(8,128)(2,1)}), bf16[32,8,512]{2,1,0:T(8,128)(2,1)S(1)}, u32[]{:S(2)}, u32[]{:S(2)}) %all-to-all-start.15) | async-done | bytes 262176 | tf_op jit(solution)/shard_map/all_to_all | solution.py:315
  294.7 0.9 copy-done.31
  295.6 1.5 shard_map.106
  297.1 3.8 %collective-permute-start.12 = (bf16[832,128]{1,0:T(8,128)(2,1)S(1)}, bf16[832,128]{1,0:T(8,128)(2,1)S(1)}, u32[]{:S(2)}, u32[]{:S(2)}) collective-permute-start(bf16[832,128]{1,0:T(8,128)(2,1)S(1)} %get-tuple-element.145), channel_id=1, source_target_pairs={{0,1},{1,0},{2,3},{3,2},{4,5},{5,4},{6,7},{7,6},{8,9},{9,8},{10,11... | collective-permute-start | bytes 638984 | tf_op jit(solution)/shard_map/ppermute | solution.py:297
  300.9 2.4 collective-permute-start.10
  303.3 2.7 collective-permute-start.11
  306.0 0.6 shard_map.107.refs_4_
  306.6 1.3 collective-permute-start.15
  307.9 1.3 collective-permute-start.14
  309.2 1.3 collective-permute-start.13
  310.6 7.9 %collective-permute-done.11.refs_3_ = bf16[1344,128]{1,0:T(8,128)(2,1)S(1)} collective-permute-done((bf16[1344,128]{1,0:T(8,128)(2,1)S(1)}, bf16[1344,128]{1,0:T(8,128)(2,1)S(1)}, u32[]{:S(2)}, u32[]{:S(2)}) %collective-permute-start.11) | collective-permute-done | bytes 344096 | tf_op jit(solution)/shard_map/ppermute | solution.py:301
  318.5 0.6 collective-permute-done.15.refs_7_
  319.1 1.2 collective-permute-done.14.refs_6_
  320.3 8.3 %collective-permute-done.13.refs_5_ = bf16[1344,128]{1,0:T(8,128)(2,1)S(1)} collective-permute-done((bf16[1344,128]{1,0:T(8,128)(2,1)S(1)}, bf16[1344,128]{1,0:T(8,128)(2,1)S(1)}, u32[]{:S(2)}, u32[]{:S(2)}) %collective-permute-start.13) | collective-permute-done | bytes 344096 | tf_op jit(solution)/shard_map/ppermute | solution.py:301
  328.6 1.7 shard_map.108
  (86 shorter events, 3.9 us)
Async XLA Ops:
  0.6 0.9 copy-start.32
  0.6 0.9 copy-start.33
  0.7 12.5 %copy-start = (bf16[4096,128]{1,0:T(8,128)(2,1)S(1)}, bf16[4096,128]{1,0:T(8,128)(2,1)}, u32[]{:S(2)}) copy-start(bf16[4096,128]{1,0:T(8,128)(2,1)} %mine_ref.3) | copy-start | bytes 3145732
  1.6 4.8 %collective-permute-start.3 = (bf16[320,128]{1,0:T(8,128)(2,1)S(1)}, bf16[320,128]{1,0:T(8,128)(2,1)S(1)}, u32[]{:S(2)}, u32[]{:S(2)}) collective-permute-start(bf16[320,128]{1,0:T(8,128)(2,1)S(1)} %maximum_maximum_fusion.refs_0_), channel_id=1, source_target_pairs={{0,192},{64,0},{128,64},{192,128},{1,193},{65,1},{129,65},{193,129... | collective-permute-start | bytes 245768 | tf_op jit(solution)/shard_map/ppermute | solution.py:301
  4.9 4.9 %collective-permute-start.2 = (bf16[320,128]{1,0:T(8,128)(2,1)S(1)}, bf16[320,128]{1,0:T(8,128)(2,1)S(1)}, u32[]{:S(2)}, u32[]{:S(2)}) collective-permute-start(bf16[320,128]{1,0:T(8,128)(2,1)S(1)} %maximum_maximum_fusion.refs_0_), channel_id=1, source_target_pairs={{0,128},{64,192},{128,0},{192,64},{1,129},{65,193},{129,1},{193,65... | collective-permute-start | bytes 245768 | tf_op jit(solution)/shard_map/ppermute | solution.py:301
  5.4 6.4 %collective-permute-start.1 = (bf16[320,128]{1,0:T(8,128)(2,1)S(1)}, bf16[320,128]{1,0:T(8,128)(2,1)S(1)}, u32[]{:S(2)}, u32[]{:S(2)}) collective-permute-start(bf16[320,128]{1,0:T(8,128)(2,1)S(1)} %maximum_maximum_fusion.refs_0_), channel_id=1, source_target_pairs={{0,64},{64,128},{128,192},{192,0},{1,65},{65,129},{129,193},{193,1... | collective-permute-start | bytes 245768 | tf_op jit(solution)/shard_map/ppermute | solution.py:301
  11.9 3.8 %collective-permute-start.4 = (bf16[4,320,128]{2,1,0:T(8,128)(2,1)S(1)}, bf16[4,320,128]{2,1,0:T(8,128)(2,1)S(1)}, u32[]{:S(2)}, u32[]{:S(2)}) collective-permute-start(bf16[4,320,128]{2,1,0:T(8,128)(2,1)S(1)} %pad_maximum_fusion), channel_id=1, source_target_pairs={{0,1},{1,0},{2,3},{3,2},{4,5},{5,4},{6,7},{7,6},{8,9},{9,8},{10,11... | collective-permute-start | bytes 983048 | tf_op jit(solution)/shard_map/ppermute | solution.py:297
  13.2 1.7 collective-permute-start.5
  14.2 4.0 %collective-permute-start = (bf16[512,128]{1,0:T(8,128)(2,1)S(1)}, bf16[512,128]{1,0:T(8,128)(2,1)S(1)}, u32[]{:S(2)}, u32[]{:S(2)}) collective-permute-start(bf16[512,128]{1,0:T(8,128)(2,1)S(1)} %constant_dynamic-slice_fusion.1), channel_id=1, source_target_pairs={{0,1},{1,0},{2,3},{3,2},{4,5},{5,4},{6,7},{7,6},{8,9},{9,8},{10,11... | collective-permute-start | bytes 393224 | tf_op jit(solution)/shard_map/ppermute | solution.py:297
  15.7 2.6 copy-start.1
  18.2 1.1 copy-start.28
  18.2 1.1 copy-start.30
  117.3 27.9 %copy-start.4 = (bf16[256,512]{1,0:T(8,128)(2,1)}, bf16[256,512]{1,0:T(8,128)(2,1)S(1)}, u32[]{:S(2)}) copy-start(bf16[256,512]{1,0:T(8,128)(2,1)S(1)} %get-tuple-element.95.x_ref) | copy-start | bytes 786436
  145.6 28.0 %copy-start.7 = (bf16[256,512]{1,0:T(8,128)(2,1)}, bf16[256,512]{1,0:T(8,128)(2,1)S(1)}, u32[]{:S(2)}) copy-start(bf16[256,512]{1,0:T(8,128)(2,1)S(1)} %get-tuple-element.101.gg_ref) | copy-start | bytes 786436
  174.1 29.4 %copy-start.9 = (bf16[256,512]{1,0:T(8,128)(2,1)}, bf16[256,512]{1,0:T(8,128)(2,1)S(1)}, u32[]{:S(2)}) copy-start(bf16[256,512]{1,0:T(8,128)(2,1)S(1)} %get-tuple-element.107.gg_ref) | copy-start | bytes 786436
  174.1 29.4 %copy-start.13 = (bf16[256,512]{1,0:T(8,128)(2,1)}, bf16[256,512]{1,0:T(8,128)(2,1)S(1)}, u32[]{:S(2)}) copy-start(bf16[256,512]{1,0:T(8,128)(2,1)S(1)} %get-tuple-element.104.y_ref) | copy-start | bytes 786436
  204.0 30.8 %copy-start.11 = (bf16[256,512]{1,0:T(8,128)(2,1)}, bf16[256,512]{1,0:T(8,128)(2,1)S(1)}, u32[]{:S(2)}) copy-start(bf16[256,512]{1,0:T(8,128)(2,1)S(1)} %get-tuple-element.113.gg_ref) | copy-start | bytes 786436
  204.0 30.7 %copy-start.15 = (bf16[256,512]{1,0:T(8,128)(2,1)}, bf16[256,512]{1,0:T(8,128)(2,1)S(1)}, u32[]{:S(2)}) copy-start(bf16[256,512]{1,0:T(8,128)(2,1)S(1)} %get-tuple-element.110.y_ref) | copy-start | bytes 786436
  234.8 0.7 copy-start.2
  235.5 0.7 copy-start.6
  236.2 0.7 copy-start.23
  236.9 0.7 copy-start.26
  237.6 35.0 %all-to-all-start.14 = ((bf16[32,8,512]{2,1,0:T(8,128)(2,1)}), bf16[32,8,512]{2,1,0:T(8,128)(2,1)S(1)}, u32[]{:S(2)}, u32[]{:S(2)}) async-start(bf16[32,8,512]{2,1,0:T(8,128)(2,1)} %copy-done.6), calls=%async_computation.14 | async-start | bytes 524288 | tf_op jit(solution)/shard_map/all_to_all | solution.py:315
  243.8 1.0 copy-start.5
  244.8 0.9 copy-start.8
  245.7 0.9 copy-start.14
  246.7 21.4 %copy-start.10 = (bf16[256,512]{1,0:T(8,128)(2,1)S(1)}, bf16[256,512]{1,0:T(8,128)(2,1)}, u32[]{:S(2)}) copy-start(bf16[256,512]{1,0:T(8,128)(2,1)} %copy-done.9) | copy-start | bytes 786436
  246.7 21.4 %copy-start.16 = (bf16[256,512]{1,0:T(8,128)(2,1)S(1)}, bf16[256,512]{1,0:T(8,128)(2,1)}, u32[]{:S(2)}) copy-start(bf16[256,512]{1,0:T(8,128)(2,1)} %copy-done.15) | copy-start | bytes 786436
  248.0 21.4 %copy-start.17 = (bf16[832,128]{1,0:T(8,128)(2,1)}, bf16[832,128]{1,0:T(8,128)(2,1)S(1)}, u32[]{:S(2)}) copy-start(bf16[832,128]{1,0:T(8,128)(2,1)S(1)} %get-tuple-element.128.refs_2_) | copy-start | bytes 638980
  248.0 21.6 %copy-start.3 = (bf16[32,8,512]{2,1,0:T(8,128)(2,1)S(1)}, bf16[32,8,512]{2,1,0:T(8,128)(2,1)}, u32[]{:S(2)}) copy-start(bf16[32,8,512]{2,1,0:T(8,128)(2,1)} %copy-done.2) | copy-start | bytes 786436
  248.0 21.6 %copy-start.12 = (bf16[256,512]{1,0:T(8,128)(2,1)S(1)}, bf16[256,512]{1,0:T(8,128)(2,1)}, u32[]{:S(2)}) copy-start(bf16[256,512]{1,0:T(8,128)(2,1)} %copy-done.11) | copy-start | bytes 786436
  248.0 21.6 %copy-start.24 = (bf16[256,512]{1,0:T(8,128)(2,1)S(1)}, bf16[256,512]{1,0:T(8,128)(2,1)}, u32[]{:S(2)}) copy-start(bf16[256,512]{1,0:T(8,128)(2,1)} %copy-done.23) | copy-start | bytes 786436
  248.1 23.5 %collective-permute-start.8 = (bf16[832,128]{1,0:T(8,128)(2,1)S(1)}, bf16[832,128]{1,0:T(8,128)(2,1)S(1)}, u32[]{:S(2)}, u32[]{:S(2)}) collective-permute-start(bf16[832,128]{1,0:T(8,128)(2,1)S(1)} %get-tuple-element.123), channel_id=1, source_target_pairs={{0,1},{1,0},{2,3},{3,2},{4,5},{5,4},{6,7},{7,6},{8,9},{9,8},{10,11... | collective-permute-start | bytes 638984 | tf_op jit(solution)/shard_map/ppermute | solution.py:297
  269.5 1.5 copy-start.21
  269.5 2.7 collective-permute-start.7
  271.0 1.7 collective-permute-start.6
  271.5 0.7 copy-start.19
  272.6 0.9 copy-start.18
  272.6 1.0 copy-start.20
  272.6 1.2 copy-start.22
  273.9 20.8 %copy-start.29 = (bf16[256,256]{1,0:T(8,128)(2,1)S(1)}, bf16[256,256]{1,0:T(8,128)(2,1)}, u32[]{:S(2)}) copy-start(bf16[256,256]{1,0:T(8,128)(2,1)} %copy-done.28) | copy-start | bytes 393220
  275.4 19.3 %copy-start.25 = (bf16[256,512]{1,0:T(8,128)(2,1)S(1)}, bf16[256,512]{1,0:T(8,128)(2,1)}, u32[]{:S(2)}) copy-start(bf16[256,512]{1,0:T(8,128)(2,1)} %copy-done.23) | copy-start | bytes 786436
  275.4 19.3 %copy-start.27 = (bf16[256,512]{1,0:T(8,128)(2,1)S(1)}, bf16[256,512]{1,0:T(8,128)(2,1)}, u32[]{:S(2)}) copy-start(bf16[256,512]{1,0:T(8,128)(2,1)} %copy-done.26) | copy-start | bytes 786436
  275.4 19.3 %all-to-all-start.15 = ((bf16[32,8,512]{2,1,0:T(8,128)(2,1)}), bf16[32,8,512]{2,1,0:T(8,128)(2,1)S(1)}, u32[]{:S(2)}, u32[]{:S(2)}) async-start(bf16[32,8,512]{2,1,0:T(8,128)(2,1)} %shard_map.104), calls=%async_computation.15 | async-start | bytes 524288 | tf_op jit(solution)/shard_map/all_to_all | solution.py:315
  285.0 24.1 %collective-permute-start.9 = (bf16[1344,128]{1,0:T(8,128)(2,1)}, bf16[1344,128]{1,0:T(8,128)(2,1)S(1)}, u32[]{:S(2)}, u32[]{:S(2)}) collective-permute-start(bf16[1344,128]{1,0:T(8,128)(2,1)} %get-tuple-element.137), channel_id=1, source_target_pairs={{0,64},{64,128},{128,192},{1,65},{65,129},{129,193},{2,66},{66,130... | collective-permute-start | bytes 1032200 | tf_op jit(solution)/shard_map/ppermute | solution.py:301
  294.7 0.9 copy-start.31
  297.1 8.9 %collective-permute-start.12 = (bf16[832,128]{1,0:T(8,128)(2,1)S(1)}, bf16[832,128]{1,0:T(8,128)(2,1)S(1)}, u32[]{:S(2)}, u32[]{:S(2)}) collective-permute-start(bf16[832,128]{1,0:T(8,128)(2,1)S(1)} %get-tuple-element.145), channel_id=1, source_target_pairs={{0,1},{1,0},{2,3},{3,2},{4,5},{5,4},{6,7},{7,6},{8,9},{9,8},{10,11... | collective-permute-start | bytes 638984 | tf_op jit(solution)/shard_map/ppermute | solution.py:297
  300.9 9.8 %collective-permute-start.10 = (bf16[1344,128]{1,0:T(8,128)(2,1)S(1)}, bf16[1344,128]{1,0:T(8,128)(2,1)S(1)}, u32[]{:S(2)}, u32[]{:S(2)}) collective-permute-start(bf16[1344,128]{1,0:T(8,128)(2,1)S(1)} %get-tuple-element.138), channel_id=1, source_target_pairs={{0,128},{64,192},{192,64},{1,129},{65,193},{193,65},{2,130},{66,19... | collective-permute-start | bytes 1032200 | tf_op jit(solution)/shard_map/ppermute | solution.py:301
  303.3 15.2 %collective-permute-start.11 = (bf16[1344,128]{1,0:T(8,128)(2,1)S(1)}, bf16[1344,128]{1,0:T(8,128)(2,1)S(1)}, u32[]{:S(2)}, u32[]{:S(2)}) collective-permute-start(bf16[1344,128]{1,0:T(8,128)(2,1)S(1)} %get-tuple-element.139), channel_id=1, source_target_pairs={{0,192},{128,64},{192,128},{1,193},{129,65},{193,129},{2,194},{130... | collective-permute-start | bytes 1032200 | tf_op jit(solution)/shard_map/ppermute | solution.py:301
  306.6 12.6 %collective-permute-start.15 = (bf16[1344,128]{1,0:T(8,128)(2,1)S(1)}, bf16[1344,128]{1,0:T(8,128)(2,1)S(1)}, u32[]{:S(2)}, u32[]{:S(2)}) collective-permute-start(bf16[1344,128]{1,0:T(8,128)(2,1)S(1)} %shard_map.107.refs_4_), channel_id=1, source_target_pairs={{64,0},{65,1},{66,2},{67,3},{68,4},{69,5},{70,6},{71,7},{72,8},{73... | collective-permute-start | bytes 1032200 | tf_op jit(solution)/shard_map/ppermute | solution.py:301
  307.9 12.5 %collective-permute-start.14 = (bf16[1344,128]{1,0:T(8,128)(2,1)S(1)}, bf16[1344,128]{1,0:T(8,128)(2,1)S(1)}, u32[]{:S(2)}, u32[]{:S(2)}) collective-permute-start(bf16[1344,128]{1,0:T(8,128)(2,1)S(1)} %shard_map.107.refs_4_), channel_id=1, source_target_pairs={{128,0},{129,1},{130,2},{131,3},{132,4},{133,5},{134,6},{135,7},{1... | collective-permute-start | bytes 1032200 | tf_op jit(solution)/shard_map/ppermute | solution.py:301
  309.2 19.4 %collective-permute-start.13 = (bf16[1344,128]{1,0:T(8,128)(2,1)S(1)}, bf16[1344,128]{1,0:T(8,128)(2,1)S(1)}, u32[]{:S(2)}, u32[]{:S(2)}) collective-permute-start(bf16[1344,128]{1,0:T(8,128)(2,1)S(1)} %shard_map.107.refs_4_), channel_id=1, source_target_pairs={{192,0},{193,1},{194,2},{195,3},{196,4},{197,5},{198,6},{199,7},{2... | collective-permute-start | bytes 1032200 | tf_op jit(solution)/shard_map/ppermute | solution.py:301
where the time goes:
time: 331 us; the launch traced here: 330 us
  blocking collectives  211 us (64%)
  starting transfers between devices  57.1 us (17%)
  waiting for transfers between devices  32.6 us (10%)
  Pallas kernels  19.3 us (6%)
  local copies, waits for them, and re-layouts  8.86 us (3%)
    all_to_all x14, blocking collectives, swap(): return lax.all_to_all(block, ('y', 'z'), 0, 0, tiled=True)  211 us
    ppermute x7, starting transfers between devices, to_other(): return lax.ppermute(value, 'c', [(0, 1), (1, 0)])  26.5 us
    ppermute x9, waiting for transfers between devices, shift(): return lax.ppermute(value, 'x', [(i, j) for i, j in route if j in targets])  23.9 us
    all_to_all x2, starting transfers between devices, swap(): return lax.all_to_all(block, ('y', 'z'), 0, 0, tiled=True)  15.9 us
    ppermute x9, starting transfers between devices, shift(): return lax.ppermute(value, 'x', [(i, j) for i, j in route if j in targets])  14.7 us
    pallas_call x10, Pallas kernels, run(): pl.pallas_call(kernel, out_shape=outs, grid_spec=pltpu.PrefetchScalarGrid...  13.6 us
    all_to_all x2, waiting for transfers between devices, swap(): return lax.all_to_all(block, ('y', 'z'), 0, 0, tiled=True)  8.36 us
    unnamed x68, local copies, waits for them, and re-layouts  7.11 us
  transfers between devices with their start and end apart: 18, of which 10 were waited for; matrix products, arithmetic and copies ran while one was open for 0% of the time, Pallas kernels for 3%

commit v1 on v0

--- a/solution.py
+++ b/solution.py
@@ -31,13 +31,16 @@
     return jnp.where(natural == c, 1.0, 0.0).astype(BF)
 
 
-def rows_of(ref):
-    d, i, n = ref.shape
-    return ref[...].astype(F32).reshape(d * i, n)
-
-
-def put_rows(ref, value):
-    ref[...] = value.reshape(ref.shape).astype(ref.dtype)
+def rows_of(ref, half=0):
+    d, _, n = ref.shape
+    return ref[:, 8 * half : 8 * half + 8, :].astype(F32).reshape(d * 8, n)
+
+
+def put_rows(ref, *values):
+    d, _, n = ref.shape
+    slabs = [v.reshape(d, 8, n) for v in values]
+    both = slabs[0] if len(slabs) == 1 else jnp.concatenate(slabs, axis=1)
+    ref[...] = both.astype(ref.dtype)
 
 
 def block_of(own_ref, other_ref, c, core, k, start, stop):
@@ -109,24 +112,46 @@
     put_rows(z_ref, nn(rt_ref[...], new))
 
 
+def mix_both_kernel(pair_ref, lt_ref, l_ref, out_ref):
+    u = nn(lt_ref[...], rows_of(pair_ref, 0).astype(BF))
+    gz = nn(l_ref[...], rows_of(pair_ref, 1).astype(BF))
+    put_rows(out_ref, u, gz)
+
+
+def top_kernel(x_ref, u_ref, gt_ref, rt_ref, y_ref, gt_top_ref, x_out, pair_ref):
+    x = x_ref[...]
+    sig = jax.nn.sigmoid(nn(gt_ref[...], x))
+    new = (x.astype(F32) + rows_of(u_ref) * sig).astype(BF)
+    x_out[...] = new
+    top = jax.nn.sigmoid(nn(gt_top_ref[...], new))
+    put_rows(pair_ref, nn(rt_ref[...], new), y_ref[...].astype(F32) * top)
+
+
 def gate_back(upper, x, u, gt, gu_ref, gg_ref):
     sig = jax.nn.sigmoid(nn(gt, x))
     put_rows(gu_ref, upper * sig)
     gg_ref[...] = (upper * u * sig * (1.0 - sig)).astype(BF)
 
 
-def back_start_kernel(y_ref, x_ref, u_ref, gt_ref, gu_ref, gg_ref):
-    gate_back(y_ref[...].astype(F32), x_ref[...], rows_of(u_ref), gt_ref[...], gu_ref, gg_ref)
-
-
-def lower_of(y_ref, gz_ref, gg_ref, r_ref, g_ref):
+def lower_of(y, gz, gg, r, g):
+    return (y.astype(F32) + nn(r, gz) + nn(g, gg)).astype(BF)
+
+
+def top_back_kernel(
+    y_ref, pair_ref, x_top_ref, gt_top_ref, r_ref, g_ref, x_ref, u_ref, gt_ref, y_out, gg_top_out, gu_ref, gg_out
+):
+    y = y_ref[...]
+    sig = jax.nn.sigmoid(nn(gt_top_ref[...], x_top_ref[...]))
+    gg = (y.astype(F32) * rows_of(pair_ref, 0) * sig * (1.0 - sig)).astype(BF)
+    gg_top_out[...] = gg
+    lower = lower_of(y, rows_of(pair_ref, 1).astype(BF), gg, r_ref[...], g_ref[...])
+    y_out[...] = lower
+    gate_back(lower.astype(F32), x_ref[...], rows_of(u_ref), gt_ref[...], gu_ref, gg_out)
+
+
+def back_kernel(y_ref, gz_ref, gg_ref, r_ref, g_ref, x_ref, u_ref, gt_ref, y_out, gu_ref, gg_out):
     gz = rows_of(gz_ref).astype(BF)
-    lower = y_ref[...].astype(F32) + nn(r_ref[...], gz)
-    return (lower + nn(g_ref[...], gg_ref[...])).astype(BF)
-
-
-def back_kernel(y_ref, gz_ref, gg_ref, r_ref, g_ref, x_ref, u_ref, gt_ref, y_out, gu_ref, gg_out):
-    lower = lower_of(y_ref, gz_ref, gg_ref, r_ref, g_ref)
+    lower = lower_of(y_ref[...], gz, gg_ref[...], r_ref[...], g_ref[...])
     y_out[...] = lower
     gate_back(lower.astype(F32), x_ref[...], rows_of(u_ref), gt_ref[...], gu_ref, gg_out)
 
@@ -156,96 +181,48 @@
     return parts
 
 
-def put_parts(core, parts, mine_out, other_out):
-    start = 0
-    for low, high in zip(*parts):
-        stop = start + low.shape[0]
-        mine_out[start:stop, :] = jnp.where(core == 0, low, high).astype(BF)
-        other_out[start:stop, :] = jnp.where(core == 0, high, low).astype(BF)
-        start = stop
-
-
-def parts_kernel(at_ref, x_ref, gz_ref, gg_ref, z_ref, gu_ref, y_ref, mine_out, other_out):
-    parts = parts_of(
-        x_ref[...],
-        rows_of(gz_ref).astype(BF),
-        gg_ref[...],
-        rows_of(z_ref).astype(BF),
-        rows_of(gu_ref).astype(BF),
-        y_ref[...],
-    )
-    put_parts(at_ref[1], parts, mine_out, other_out)
-
-
-def last_kernel(
-    at_ref, x_ref, gz_ref, gg_ref, z_ref, gu_ref, y_ref, r_ref, g_ref, mine_out, other_out
-):
-    lower = lower_of(y_ref, gz_ref, gg_ref, r_ref, g_ref)
-    parts = parts_of(
-        x_ref[...],
-        rows_of(gz_ref).astype(BF),
-        gg_ref[...],
-        rows_of(z_ref).astype(BF),
-        rows_of(gu_ref).astype(BF),
-        lower,
-    )
-    put_parts(at_ref[1], parts, mine_out, other_out)
-
-
-def join(core, mine_ref, other_ref, out_ref):
-    n = (out_ref.shape[0] - 320) // 2
-    out_ref[pl.ds(pl.multiple_of(core * n, n), n), :] = mine_ref[:n, :]
-    out_ref[pl.ds(pl.multiple_of((1 - core) * n, n), n), :] = other_ref[:n, :]
-    total = mine_ref[n:, :].astype(F32) + other_ref[n:, :].astype(F32)
-    out_ref[2 * n :, :] = total.astype(BF)
-
-
-def join_kernel(at_ref, mine_ref, other_ref, out_ref):
-    join(at_ref[1], mine_ref, other_ref, out_ref)
-
-
-def route_kernel(at_ref, *refs):
-    sect, core = at_ref[0], at_ref[1]
-    mine, other, outs = refs[:3], refs[3:6], refs[6:]
-    for k in range(4):
-        target = lax.rem(sect + k, 4)
-
-        @pl.when(target == 0)
-        def _():
-            outs[k][...] = jnp.zeros_like(outs[k])
-
-        for layer in range(1, 4):
-
-            @pl.when(target == layer)
-            def _():
-                join(core, mine[layer - 1], other[layer - 1], outs[k])
-
-
-def settle_kernel(at_ref, *refs):
-    early, late = refs[:4], refs[4:8]
-    y_out, r_out, g_out, l_out = refs[8:]
-    sect = at_ref[0]
-    n = y_out.shape[0] // 4
-
-    def settle(parts):
-        total = None
-        for k in range(4):
-            source = pl.multiple_of(lax.rem(sect - k + 4, 4) * n, n)
-            y_out[pl.ds(source, n), :] = parts[k][:n, :]
-            part = parts[k][n:, :].astype(F32)
-            total = part if total is None else total + part
-        r_out[...] = total[:128]
-        g_out[...] = total[128:256]
-        l_out[0] = total[256:, :64]
-        l_out[1] = total[256:, 64:]
-
-    @pl.when(sect == 0)
-    def _():
-        settle(late)
-
-    @pl.when(sect != 0)
-    def _():
-        settle(early)
+def put_parts(parts, out_ref):
+    for c in range(2):
+        start = 0
+        for part in parts[c]:
+            stop = start + part.shape[0]
+            out_ref[0, c, start:stop, :] = part.astype(BF)
+            start = stop
+
+
+def top_parts_kernel(x_ref, gave_ref, gg_ref, took_ref, y_ref, out_ref):
+    gz = rows_of(gave_ref, 1).astype(BF)
+    z = rows_of(took_ref, 0).astype(BF)
+    gu = rows_of(took_ref, 1).astype(BF)
+    put_parts(parts_of(x_ref[...], gz, gg_ref[...], z, gu, y_ref[...]), out_ref)
+
+
+def parts_kernel(x_ref, gz_ref, gg_ref, z_ref, gu_ref, y_ref, held_ref, out_ref):
+    gz = rows_of(gz_ref).astype(BF)
+    z = rows_of(z_ref).astype(BF)
+    gu = rows_of(gu_ref).astype(BF)
+    put_parts(parts_of(x_ref[...], gz, gg_ref[...], z, gu, y_ref[...]), out_ref)
+
+
+def last_kernel(x_ref, gz_ref, gg_ref, z_ref, gu_ref, y_ref, r_ref, g_ref, held_ref, out_ref):
+    gz = rows_of(gz_ref).astype(BF)
+    z = rows_of(z_ref).astype(BF)
+    gu = rows_of(gu_ref).astype(BF)
+    lower = lower_of(y_ref[...], gz, gg_ref[...], r_ref[...], g_ref[...])
+    put_parts(parts_of(x_ref[...], gz, gg_ref[...], z, gu, lower), out_ref)
+
+
+def settle_kernel(got_ref, y_out, r_out, g_out, l_out):
+    n = y_out.shape[0] // 8
+    total = None
+    for i in range(8):
+        y_out[n * i : n * i + n, :] = got_ref[i, :n, :]
+        part = got_ref[i, n:, :].astype(F32)
+        total = part if total is None else total + part
+    r_out[...] = total[:128]
+    g_out[...] = total[128:256]
+    l_out[0] = total[256:, :64]
+    l_out[1] = total[256:, 64:]
 
 
 def run(kernel, outs, *args, dots=1, at=None, scratch=(), blocks=None):
@@ -282,6 +259,25 @@
     )(at, *args)
 
 
+def run_parts(kernel, layer, whole, *args):
+    more = {} if layer == 3 else {"input_output_aliases": {len(args) - 1: 0}}
+    specs = [pl.BlockSpec(a.shape, lambda i, nd=a.ndim: (0,) * nd) for a in args]
+    if layer != 3:
+        specs[-1] = pl.BlockSpec(memory_space=pl.ANY)
+    return pl.pallas_call(
+        kernel,
+        out_shape=whole,
+        grid=(1,),
+        in_specs=specs,
+        out_specs=pl.BlockSpec((1,) + whole.shape[1:], lambda i: (layer, 0, 0, 0)),
+        compiler_params=pltpu.CompilerParams(vmem_limit_bytes=16 << 20),
+        cost_estimate=pl.CostEstimate(
+            flops=18 * 256 * 256 * 512, bytes_accessed=3 << 20, transcendentals=0
+        ),
+        **more,
+    )(*args)
+
+
 def sds(*shape, dtype=BF):
     return jax.ShapeDtypeStruct(shape, dtype)
 
@@ -296,9 +292,8 @@
     def to_other(value):
         return lax.ppermute(value, "c", [(0, 1), (1, 0)])
 
-    def shift(value, k, targets=range(4)):
-        route = [(i, (i + k) % sections) for i in range(sections)]
-        return lax.ppermute(value, "x", [(i, j) for i, j in route if j in targets])
+    def shift(value, k):
+        return lax.ppermute(value, "x", [(i, (i + k) % sections) for i in range(sections)])
 
     l_flat = jnp.concatenate([l_weight[0, 0], l_weight[0, 1]], axis=1)
     packed = jnp.concatenate([r_weight[0, 0], g_weight[0, 0], l_flat], axis=0)
@@ -342,28 +337,49 @@
     z, y = lax.optimization_barrier((z, y))
     x = [x0]
     z_all, u_all = [], []
-    for s in range(sections):
+    last = sections - 1
+    pair = sds(32, 16, tokens)
+    for s in range(last):
         z = swap(z)
         z_all.append(z)
         u = swap(run(mix_kernel, sent, z, mats[s][5]))
         u_all.append(u)
-        if s + 1 < sections:
+        if s + 1 < last:
             new, z = run(gated_kernel, [flat, sent], x[s], u, mats[s][3], mats[s + 1][1], dots=2)
-            x.append(new)
-    last = sections - 1
-    gu, gg = run(back_start_kernel, [sent, flat], y, x[last], u_all[last], mats[last][3])
-    rows = sds(tokens + 320, 128)
-    joined = sds(2 * tokens + 320, 128)
-    kept, crossed = [], []
-    for s in range(last, -1, -1):
+        else:
+            new, both = run(
+                top_kernel,
+                [flat, pair],
+                x[s],
+                u,
+                mats[s][3],
+                mats[last][1],
+                y,
+                mats[last][3],
+                dots=3,
+            )
+        x.append(new)
+    took = swap(both)
+    gave = swap(run(mix_both_kernel, pair, took, mats[last][5], mats[last][4], dots=2))
+    y, gg_top, gu, gg = run(
+        top_back_kernel,
+        [flat, flat, sent, flat],
+        y,
+        gave,
+        x[last],
+        mats[last][3],
+        mats[last][0],
+        mats[last][2],
+        x[last - 1],
+        u_all[last - 1],
+        mats[last - 1][3],
+        dots=4,
+    )
+    whole = sds(sections, 2, tokens + 320, 128)
+    parts = run_parts(top_parts_kernel, last, whole, x[last], gave, gg_top, took, y)
+    for s in range(last - 1, -1, -1):
         gu = swap(gu)
-        if s == 0:
-            gu, kept, crossed = lax.optimization_barrier((gu, kept, crossed))
-        mixed = run(mix_kernel, sent, gu, mats[s][4])
-        if s == 0:
-            routed = run(route_kernel, [joined] * 4, *kept, *crossed, at=at)
-            mixed, routed = lax.optimization_barrier((mixed, routed))
-        gz = swap(mixed)
+        gz = swap(run(mix_kernel, sent, gu, mats[s][4]))
         held = (x[s], gz, gg, z_all[s], gu)
         if s > 0:
             y, gu, gg = run(
@@ -379,17 +395,11 @@
                 mats[s - 1][3],
                 dots=3,
             )
-            part, away = run(parts_kernel, [rows, rows], *held, y, at=at, dots=9)
-            kept.insert(0, part)
-            crossed.insert(0, to_other(away))
-    early = [routed[0]]
-    for k in range(1, sections):
-        early.append(shift(routed[k], k, (1, 2, 3)))
-    part, away = run(
-        last_kernel, [rows, rows], *held, y, mats[0][0], mats[0][2], at=at, dots=11
-    )
-    final = run(join_kernel, joined, part, to_other(away), at=at)
-    late = [final] + [shift(final, k, (0,)) for k in range(1, sections)]
+            parts = run_parts(parts_kernel, s, whole, *held, y, parts)
+    parts = run_parts(last_kernel, 0, whole, *held, y, mats[0][0], mats[0][2], parts)
+    got = lax.all_to_all(
+        parts.reshape(sections * 2, tokens + 320, 128), ("x", "c"), 0, 0, tiled=True
+    )
     y_out, r_grad, g_grad, l_grad = run(
         settle_kernel,
         [
@@ -398,9 +408,7 @@
             sds(128, 128, dtype=F32),
             sds(2, 64, 64, dtype=F32),
         ],
-        *early,
-        *late,
-        at=at,
+        got,
     )
     return y_out[None], r_grad[None, None], g_grad[None, None], l_grad[None]
 

time: 331 us -> 301 us (0.909)
  starting transfers between devices: 57.1 us -> 12.5 us
  blocking collectives: 211 us -> 244 us
  waiting for transfers between devices: 32.6 us -> 8.21 us
  local copies, waits for them, and re-layouts: 8.86 us -> 16 us
  Pallas kernels: 19.3 us -> 15.2 us
    all_to_all x0 -> x1, blocking collectives: none -> 44.5 us  [program(): lax.all_to_all(parts.reshape(sections * 2, tokens + 320, 128), ('x', 'c')...]
    ppermute x7 -> x3, starting transfers between devices: 26.5 us -> 2.89 us  [to_other(): return lax.ppermute(value, 'c', [(0, 1), (1, 0)])]
    ppermute x9 -> x3, waiting for transfers between devices: 23.9 us -> 3.16 us  [shift(): lax.ppermute(value, 'x', [(i, (i + k) % sections) for i in range(sections)])]
    all_to_all x2 -> x1, starting transfers between devices: 15.9 us -> 4.6 us  [swap(): return lax.all_to_all(block, ('y', 'z'), 0, 0, tiled=True)]
    all_to_all x14 -> x13, blocking collectives: 211 us -> 200 us  [swap(): return lax.all_to_all(block, ('y', 'z'), 0, 0, tiled=True)]
    ppermute x9 -> x3, starting transfers between devices: 14.7 us -> 5.06 us  [shift(): lax.ppermute(value, 'x', [(i, (i + k) % sections) for i in range(sections)])]
    pallas_call x10 -> x3, Pallas kernels: 13.6 us -> 4.38 us  [run(): pl.pallas_call(kernel, out_shape=outs, grid_spec=pltpu.PrefetchScalarGrid...]
    unnamed x68 -> x78, local copies, waits for them, and re-layouts: 7.11 us -> 13.4 us
  transfers between devices with their start and end apart: 18 -> 7, of which waited for: 10 -> 2; matrix products, arithmetic and copies ran while one was open for 0% -> 1% of each run, Pallas kernels for 3% -> 2%
where the time goes in v1:
time: 301 us; the launch traced here: 299 us
  blocking collectives  244 us (81%)
  local copies, waits for them, and re-layouts  16 us (5%)
  Pallas kernels  15.2 us (5%)
  starting transfers between devices  12.5 us (4%)
  waiting for transfers between devices  8.21 us (3%)
    all_to_all x13, blocking collectives, swap(): return lax.all_to_all(block, ('y', 'z'), 0, 0, tiled=True)  200 us
    all_to_all x1, blocking collectives, program(): lax.all_to_all(parts.reshape(sections * 2, tokens + 320, 128), ('x', 'c')...  44.5 us
    unnamed x78, local copies, waits for them, and re-layouts  13.4 us
    pallas_call x14, Pallas kernels, run(): pl.pallas_call(kernel, out_shape=outs, compiler_params=params, cost_estim...  6.58 us
  transfers between devices with their start and end apart: 7, of which 2 were waited for; matrix products, arithmetic and copies ran while one was open for 1% of the time, Pallas kernels for 2%

profile of v1, /device:TPU:1, one launch (start us, length us, event | category | flops | bytes accessed | tf_op | source)
XLA Modules:
  0.0 299.4 jit_solution(5248926977493799865)
XLA Ops:
  0.6 0.8 slice_bitcast_fusion.1
  1.5 0.9 maximum_maximum_fusion.refs_0_
  2.3 3.3 %collective-permute-start.3 = (bf16[320,128]{1,0:T(8,128)(2,1)S(1)}, bf16[320,128]{1,0:T(8,128)(2,1)S(1)}, u32[]{:S(2)}, u32[]{:S(2)}) collective-permute-start(bf16[320,128]{1,0:T(8,128)(2,1)S(1)} %maximum_maximum_fusion.refs_0_), channel_id=1, source_target_pairs={{0,192},{64,0},{128,64},{192,128},{1,193},{65,1},{129,65},{193,129... | collective-permute-start | bytes 245768 | tf_op jit(solution)/shard_map/ppermute | solution.py:296
  5.7 1.7 collective-permute-start.2
  7.4 0.9 fusion
  8.2 3.2 %collective-permute-done.1.refs_1_ = bf16[320,128]{1,0:T(8,128)(2,1)S(1)} collective-permute-done((bf16[320,128]{1,0:T(8,128)(2,1)S(1)}, bf16[320,128]{1,0:T(8,128)(2,1)S(1)}, u32[]{:S(2)}, u32[]{:S(2)}) %collective-permute-start.1) | collective-permute-done | bytes 81952 | tf_op jit(solution)/shard_map/ppermute | solution.py:296
  11.5 2.2 collective-permute-start.4
  13.7 0.9 constant_dynamic-slice_fusion
  14.7 0.9 constant_dynamic-slice_fusion.1
  15.6 0.6 collective-permute-start
  16.3 0.8 shard_map.86.y_ref
  17.1 2.5 shard_map.84
  19.7 1.0 shard_map.85
  20.7 21.3 %all_to_all.75.z_ref = bf16[32,8,512]{2,1,0:T(8,128)(2,1)S(1)} all-to-all(bf16[32,8,512]{2,1,0:T(8,128)(2,1)S(1)} %get-tuple-element.56), channel_id=1, replica_groups=mesh['x'=4,'y'=4,'z'=8,'c'=2] {'y','z'}, dimensions={0} | all-to-all | bytes 524288 | tf_op jit(solution)/shard_map/all_to_all | solution.py:310
  42.0 0.2 shard_map.87
  42.2 15.9 %all_to_all.76.u_ref = bf16[32,8,512]{2,1,0:T(8,128)(2,1)S(1)} all-to-all(bf16[32,8,512]{2,1,0:T(8,128)(2,1)S(1)} %shard_map.87), channel_id=1, replica_groups=mesh['x'=4,'y'=4,'z'=8,'c'=2] {'y','z'}, dimensions={0} | all-to-all | bytes 524288 | tf_op jit(solution)/shard_map/all_to_all | solution.py:310
  58.1 0.5 shard_map.88
  58.6 15.6 %all_to_all.77.z_ref = bf16[32,8,512]{2,1,0:T(8,128)(2,1)S(1)} all-to-all(bf16[32,8,512]{2,1,0:T(8,128)(2,1)S(1)} %get-tuple-element.61), channel_id=1, replica_groups=mesh['x'=4,'y'=4,'z'=8,'c'=2] {'y','z'}, dimensions={0} | all-to-all | bytes 524288 | tf_op jit(solution)/shard_map/all_to_all | solution.py:310
  74.2 0.2 shard_map.89
  74.4 0.7 copy-done
  75.1 14.9 %all_to_all.78.u_ref = bf16[32,8,512]{2,1,0:T(8,128)(2,1)S(1)} all-to-all(bf16[32,8,512]{2,1,0:T(8,128)(2,1)S(1)} %shard_map.89), channel_id=1, replica_groups=mesh['x'=4,'y'=4,'z'=8,'c'=2] {'y','z'}, dimensions={0} | all-to-all | bytes 524288 | tf_op jit(solution)/shard_map/all_to_all | solution.py:310
  90.1 0.5 shard_map.90
  90.5 14.2 %all_to_all.79.z_ref = bf16[32,8,512]{2,1,0:T(8,128)(2,1)S(1)} all-to-all(bf16[32,8,512]{2,1,0:T(8,128)(2,1)S(1)} %get-tuple-element.66), channel_id=1, replica_groups=mesh['x'=4,'y'=4,'z'=8,'c'=2] {'y','z'}, dimensions={0} | all-to-all | bytes 524288 | tf_op jit(solution)/shard_map/all_to_all | solution.py:310
  104.7 0.2 shard_map.91
  105.0 0.7 copy-done.2
  105.7 14.0 %all_to_all.80.u_ref = bf16[32,8,512]{2,1,0:T(8,128)(2,1)S(1)} all-to-all(bf16[32,8,512]{2,1,0:T(8,128)(2,1)S(1)} %shard_map.91), channel_id=1, replica_groups=mesh['x'=4,'y'=4,'z'=8,'c'=2] {'y','z'}, dimensions={0} | all-to-all | bytes 524288 | tf_op jit(solution)/shard_map/all_to_all | solution.py:310
  119.7 0.5 shard_map.92
  120.2 15.7 %all_to_all.81.pair_ref.took_ref = bf16[32,16,512]{2,1,0:T(8,128)(2,1)S(1)} all-to-all(bf16[32,16,512]{2,1,0:T(8,128)(2,1)S(1)} %get-tuple-element.71), channel_id=1, replica_groups=mesh['x'=4,'y'=4,'z'=8,'c'=2] {'y','z'}, dimensions={0} | all-to-all | bytes 1048576 | tf_op jit(solution)/shard_map/all_to_all | solution.py:310
  135.9 0.3 shard_map.93
  136.2 16.8 %all_to_all.82.pair_ref.gave_ref = bf16[32,16,512]{2,1,0:T(8,128)(2,1)S(1)} all-to-all(bf16[32,16,512]{2,1,0:T(8,128)(2,1)S(1)} %shard_map.93), channel_id=1, replica_groups=mesh['x'=4,'y'=4,'z'=8,'c'=2] {'y','z'}, dimensions={0} | all-to-all | bytes 1048576 | tf_op jit(solution)/shard_map/all_to_all | solution.py:310
  153.0 0.7 shard_map.94
  153.7 0.7 copy-done.31
  154.4 14.9 %all_to_all.83.z_ref.gu_ref = bf16[32,8,512]{2,1,0:T(8,128)(2,1)S(1)} all-to-all(bf16[32,8,512]{2,1,0:T(8,128)(2,1)S(1)} %get-tuple-element.78), channel_id=1, replica_groups=mesh['x'=4,'y'=4,'z'=8,'c'=2] {'y','z'}, dimensions={0} | all-to-all | bytes 524288 | tf_op jit(solution)/shard_map/all_to_all | solution.py:310
  169.4 0.2 shard_map.95
  169.6 0.7 copy-done.4
  170.3 13.8 %all_to_all.84.gz_ref = bf16[32,8,512]{2,1,0:T(8,128)(2,1)S(1)} all-to-all(bf16[32,8,512]{2,1,0:T(8,128)(2,1)S(1)} %shard_map.95), channel_id=1, replica_groups=mesh['x'=4,'y'=4,'z'=8,'c'=2] {'y','z'}, dimensions={0} | all-to-all | bytes 524288 | tf_op jit(solution)/shard_map/all_to_all | solution.py:310
  184.1 0.5 shard_map.96
  184.7 14.0 %all_to_all.85.z_ref.gu_ref = bf16[32,8,512]{2,1,0:T(8,128)(2,1)S(1)} all-to-all(bf16[32,8,512]{2,1,0:T(8,128)(2,1)S(1)} %get-tuple-element.84), channel_id=1, replica_groups=mesh['x'=4,'y'=4,'z'=8,'c'=2] {'y','z'}, dimensions={0} | all-to-all | bytes 524288 | tf_op jit(solution)/shard_map/all_to_all | solution.py:310
  198.7 0.2 shard_map.97
  198.9 0.7 copy-done.8
  199.6 14.2 %all_to_all.86.gz_ref = bf16[32,8,512]{2,1,0:T(8,128)(2,1)S(1)} all-to-all(bf16[32,8,512]{2,1,0:T(8,128)(2,1)S(1)} %shard_map.97), channel_id=1, replica_groups=mesh['x'=4,'y'=4,'z'=8,'c'=2] {'y','z'}, dimensions={0} | all-to-all | bytes 524288 | tf_op jit(solution)/shard_map/all_to_all | solution.py:310
  213.8 0.5 shard_map.98
  214.3 0.2 copy-done.12
  214.5 0.7 copy-done.18
  215.2 0.7 copy-done.33
  215.9 14.7 %all_to_all.87.z_ref.gu_ref = bf16[32,8,512]{2,1,0:T(8,128)(2,1)S(1)} all-to-all(bf16[32,8,512]{2,1,0:T(8,128)(2,1)S(1)} %get-tuple-element.89), channel_id=1, replica_groups=mesh['x'=4,'y'=4,'z'=8,'c'=2] {'y','z'}, dimensions={0} | all-to-all | bytes 524288 | tf_op jit(solution)/shard_map/all_to_all | solution.py:310
  230.6 0.9 shard_map.99
  231.6 0.7 copy-done.6
  232.3 4.6 %all-to-all-start.13 = ((bf16[32,8,512]{2,1,0:T(8,128)(2,1)}), bf16[32,8,512]{2,1,0:T(8,128)(2,1)}, u32[]{:S(2)}, u32[]{:S(2)}) async-start(bf16[32,8,512]{2,1,0:T(8,128)(2,1)} %shard_map.99), calls=%async_computation.13 | async-start | bytes 524288 | tf_op jit(solution)/shard_map/all_to_all | solution.py:310
  236.9 0.9 copy-done.24
  237.8 0.9 copy-done.30
  238.8 0.9 copy-done.32
  239.8 0.8 shard_map.100.held_ref
  241.1 0.8 shard_map.101.held_ref
  241.9 0.1 copy-done.1
  242.3 0.8 shard_map.102.held_ref
  243.1 5.0 %all-to-all-done.13.gz_ref = bf16[32,8,512]{2,1,0:T(8,128)(2,1)} async-done(((bf16[32,8,512]{2,1,0:T(8,128)(2,1)}), bf16[32,8,512]{2,1,0:T(8,128)(2,1)}, u32[]{:S(2)}, u32[]{:S(2)}) %all-to-all-start.13) | async-done | bytes 262176 | tf_op jit(solution)/shard_map/all_to_all | solution.py:310
  248.2 0.9 copy-done.20
  249.1 0.9 copy-done.34
  250.1 0.9 copy-done.36
  251.0 0.9 copy-done.38
  251.9 1.9 shard_map.103
  253.8 44.5 %all_to_all.88.got_ref = bf16[8,832,128]{2,1,0:T(8,128)(2,1)S(1)} all-to-all(bf16[8,832,128]{2,1,0:T(8,128)(2,1)S(1)} %bitcast.19), channel_id=1, replica_groups=mesh['x'=4,'y'=4,'z'=8,'c'=2] {'x','c'}, dimensions={0} | all-to-all | bytes 3407872 | tf_op jit(solution)/shard_map/all_to_all | solution.py:400
  298.3 1.1 shard_map.104
  (70 shorter events, 1.2 us)
Async XLA Ops:
  0.6 15.6 %copy-start.16 = (bf16[4096,128]{1,0:T(8,128)(2,1)S(1)}, bf16[4096,128]{1,0:T(8,128)(2,1)}, u32[]{:S(2)}) copy-start(bf16[4096,128]{1,0:T(8,128)(2,1)} %mine_ref.3) | copy-start | bytes 3145732
  2.3 5.9 %collective-permute-start.3 = (bf16[320,128]{1,0:T(8,128)(2,1)S(1)}, bf16[320,128]{1,0:T(8,128)(2,1)S(1)}, u32[]{:S(2)}, u32[]{:S(2)}) collective-permute-start(bf16[320,128]{1,0:T(8,128)(2,1)S(1)} %maximum_maximum_fusion.refs_0_), channel_id=1, source_target_pairs={{0,192},{64,0},{128,64},{192,128},{1,193},{65,1},{129,65},{193,129... | collective-permute-start | bytes 245768 | tf_op jit(solution)/shard_map/ppermute | solution.py:296
  5.6 5.8 %collective-permute-start.1 = (bf16[320,128]{1,0:T(8,128)(2,1)S(1)}, bf16[320,128]{1,0:T(8,128)(2,1)S(1)}, u32[]{:S(2)}, u32[]{:S(2)}) collective-permute-start(bf16[320,128]{1,0:T(8,128)(2,1)S(1)} %maximum_maximum_fusion.refs_0_), channel_id=1, source_target_pairs={{0,64},{64,128},{128,192},{192,0},{1,65},{65,129},{129,193},{193,1... | collective-permute-start | bytes 245768 | tf_op jit(solution)/shard_map/ppermute | solution.py:296
  5.7 5.8 %collective-permute-start.2 = (bf16[320,128]{1,0:T(8,128)(2,1)S(1)}, bf16[320,128]{1,0:T(8,128)(2,1)S(1)}, u32[]{:S(2)}, u32[]{:S(2)}) collective-permute-start(bf16[320,128]{1,0:T(8,128)(2,1)S(1)} %maximum_maximum_fusion.refs_0_), channel_id=1, source_target_pairs={{0,128},{64,192},{128,0},{192,64},{1,129},{65,193},{129,1},{193,65... | collective-permute-start | bytes 245768 | tf_op jit(solution)/shard_map/ppermute | solution.py:296
  11.5 5.7 %collective-permute-start.4 = (bf16[4,320,128]{2,1,0:T(8,128)(2,1)S(1)}, bf16[4,320,128]{2,1,0:T(8,128)(2,1)S(1)}, u32[]{:S(2)}, u32[]{:S(2)}) collective-permute-start(bf16[4,320,128]{2,1,0:T(8,128)(2,1)S(1)} %pad_maximum_fusion), channel_id=1, source_target_pairs={{0,1},{1,0},{2,3},{3,2},{4,5},{5,4},{6,7},{7,6},{8,9},{9,8},{10,11... | collective-permute-start | bytes 983048 | tf_op jit(solution)/shard_map/ppermute | solution.py:293
  14.6 1.7 collective-permute-start.5
  15.6 4.1 %collective-permute-start = (bf16[512,128]{1,0:T(8,128)(2,1)S(1)}, bf16[512,128]{1,0:T(8,128)(2,1)S(1)}, u32[]{:S(2)}, u32[]{:S(2)}) collective-permute-start(bf16[512,128]{1,0:T(8,128)(2,1)S(1)} %constant_dynamic-slice_fusion.1), channel_id=1, source_target_pairs={{0,1},{1,0},{2,3},{3,2},{4,5},{5,4},{6,7},{7,6},{8,9},{9,8},{10,11... | collective-permute-start | bytes 393224 | tf_op jit(solution)/shard_map/ppermute | solution.py:293
  17.1 2.6 copy-start.17
  19.6 38.9 %copy-start.35 = (bf16[256,256]{1,0:T(8,128)(2,1)}, bf16[256,256]{1,0:T(8,128)(2,1)S(1)}, u32[]{:S(2)}) copy-start(bf16[256,256]{1,0:T(8,128)(2,1)S(1)} %get-tuple-element.93.r_ref) | copy-start | bytes 393220
  19.6 38.9 %copy-start.37 = (bf16[256,256]{1,0:T(8,128)(2,1)}, bf16[256,256]{1,0:T(8,128)(2,1)S(1)}, u32[]{:S(2)}) copy-start(bf16[256,256]{1,0:T(8,128)(2,1)S(1)} %get-tuple-element.94.g_ref) | copy-start | bytes 393220
  74.4 0.7 copy-start
  90.5 62.5 %copy-start.14 = (bf16[256,512]{1,0:T(8,128)(2,1)}, bf16[256,512]{1,0:T(8,128)(2,1)S(1)}, u32[]{:S(2)}) copy-start(bf16[256,512]{1,0:T(8,128)(2,1)S(1)} %get-tuple-element.65.x_ref) | copy-start | bytes 786436
  105.0 0.7 copy-start.2
  120.2 32.8 %copy-start.29 = (bf16[256,512]{1,0:T(8,128)(2,1)}, bf16[256,512]{1,0:T(8,128)(2,1)S(1)}, u32[]{:S(2)}) copy-start(bf16[256,512]{1,0:T(8,128)(2,1)S(1)} %get-tuple-element.74.x_top_ref.x_ref) | copy-start | bytes 786436
  153.7 0.7 copy-start.31
  154.4 30.2 %copy-start.21 = (bf16[256,512]{1,0:T(8,128)(2,1)}, bf16[256,512]{1,0:T(8,128)(2,1)S(1)}, u32[]{:S(2)}) copy-start(bf16[256,512]{1,0:T(8,128)(2,1)S(1)} %get-tuple-element.80.gg_ref) | copy-start | bytes 786436
  154.4 30.2 %copy-start.23 = (bf16[256,512]{1,0:T(8,128)(2,1)}, bf16[256,512]{1,0:T(8,128)(2,1)S(1)}, u32[]{:S(2)}) copy-start(bf16[256,512]{1,0:T(8,128)(2,1)S(1)} %get-tuple-element.77.y_ref) | copy-start | bytes 786436
  169.6 0.7 copy-start.4
  184.1 29.7 %copy-start.10 = (bf16[32,8,512]{2,1,0:T(8,128)(2,1)}, bf16[32,8,512]{2,1,0:T(8,128)(2,1)S(1)}, u32[]{:S(2)}) copy-start(bf16[32,8,512]{2,1,0:T(8,128)(2,1)S(1)} %all_to_all.84.gz_ref) | copy-start | bytes 786436
  184.7 29.6 %copy-start.25 = (bf16[256,512]{1,0:T(8,128)(2,1)}, bf16[256,512]{1,0:T(8,128)(2,1)S(1)}, u32[]{:S(2)}) copy-start(bf16[256,512]{1,0:T(8,128)(2,1)S(1)} %get-tuple-element.86.gg_ref) | copy-start | bytes 786436
  184.7 29.6 %copy-start.27 = (bf16[256,512]{1,0:T(8,128)(2,1)}, bf16[256,512]{1,0:T(8,128)(2,1)S(1)}, u32[]{:S(2)}) copy-start(bf16[256,512]{1,0:T(8,128)(2,1)S(1)} %get-tuple-element.83.y_ref) | copy-start | bytes 786436
  198.9 0.7 copy-start.8
  213.8 0.7 copy-start.12
  214.5 0.7 copy-start.18
  215.2 0.7 copy-start.33
  231.6 0.7 copy-start.6
  232.3 15.9 %all-to-all-start.13 = ((bf16[32,8,512]{2,1,0:T(8,128)(2,1)}), bf16[32,8,512]{2,1,0:T(8,128)(2,1)}, u32[]{:S(2)}, u32[]{:S(2)}) async-start(bf16[32,8,512]{2,1,0:T(8,128)(2,1)} %shard_map.99), calls=%async_computation.13 | async-start | bytes 524288 | tf_op jit(solution)/shard_map/all_to_all | solution.py:310
  236.9 1.0 copy-start.24
  237.8 0.9 copy-start.30
  238.8 0.9 copy-start.32
  239.7 0.9 copy-start.3
  239.7 1.0 copy-start.5
  239.7 1.1 copy-start.11
  239.7 1.2 copy-start.15
  239.7 1.3 copy-start.22
  239.7 1.3 copy-start.28
  241.1 0.9 copy-start.1
  241.1 1.0 copy-start.9
  241.1 1.1 copy-start.13
  241.1 1.2 copy-start.19
  241.1 1.3 copy-start.26
  242.3 5.8 %copy-start.7 = (bf16[32,8,512]{2,1,0:T(8,128)(2,1)S(1)}, bf16[32,8,512]{2,1,0:T(8,128)(2,1)}, u32[]{:S(2)}) copy-start(bf16[32,8,512]{2,1,0:T(8,128)(2,1)} %copy-done.6) | copy-start | bytes 786436
  248.2 1.0 copy-start.20
  249.1 0.9 copy-start.34
  250.1 0.9 copy-start.36
  251.0 0.9 copy-start.38

commit v2 on v1

--- a/solution.py
+++ b/solution.py
@@ -90,10 +90,6 @@
     return (nt(p, mine_ref[...]) + nt(o, other_ref[...])).astype(BF)
 
 
-def turn_kernel(at_ref, mine_ref, other_ref, o_ref):
-    o_ref[...] = turned(at_ref[1], mine_ref, other_ref)
-
-
 def first_kernel(at_ref, mine_ref, other_ref, rt_ref, x_ref, z_ref):
     x = turned(at_ref[1], mine_ref, other_ref)
     x_ref[...] = x
@@ -118,13 +114,17 @@
     put_rows(out_ref, u, gz)
 
 
-def top_kernel(x_ref, u_ref, gt_ref, rt_ref, y_ref, gt_top_ref, x_out, pair_ref):
+def top_kernel(
+    at_ref, x_ref, u_ref, gt_ref, rt_ref, mine_ref, other_ref, gt_top_ref, x_out, pair_ref, y_out
+):
     x = x_ref[...]
     sig = jax.nn.sigmoid(nn(gt_ref[...], x))
     new = (x.astype(F32) + rows_of(u_ref) * sig).astype(BF)
     x_out[...] = new
     top = jax.nn.sigmoid(nn(gt_top_ref[...], new))
-    put_rows(pair_ref, nn(rt_ref[...], new), y_ref[...].astype(F32) * top)
+    y = turned(at_ref[1], mine_ref, other_ref)
+    y_out[...] = y
+    put_rows(pair_ref, nn(rt_ref[...], new), y.astype(F32) * top)
 
 
 def gate_back(upper, x, u, gt, gu_ref, gg_ref):
@@ -333,8 +333,7 @@
         blocks=[mine, None, None],
     )
     crossed = sent_over(cotangent)
-    y = run(turn_kernel, flat, cotangent, crossed, at=at, blocks=[mine, None])
-    z, y = lax.optimization_barrier((z, y))
+    z, crossed = lax.optimization_barrier((z, crossed))
     x = [x0]
     z_all, u_all = [], []
     last = sections - 1
@@ -347,16 +346,19 @@
         if s + 1 < last:
             new, z = run(gated_kernel, [flat, sent], x[s], u, mats[s][3], mats[s + 1][1], dots=2)
         else:
-            new, both = run(
+            new, both, y = run(
                 top_kernel,
-                [flat, pair],
+                [flat, pair, flat],
                 x[s],
                 u,
                 mats[s][3],
                 mats[last][1],
-                y,
+                cotangent,
+                crossed,
                 mats[last][3],
-                dots=3,
+                dots=4,
+                at=at,
+                blocks=[None, None, None, None, mine, None, None],
             )
         x.append(new)
     took = swap(both)
@@ -378,6 +380,7 @@
     whole = sds(sections, 2, tokens + 320, 128)
     parts = run_parts(top_parts_kernel, last, whole, x[last], gave, gg_top, took, y)
     for s in range(last - 1, -1, -1):
+        gu, parts = lax.optimization_barrier((gu, parts))
         gu = swap(gu)
         gz = swap(run(mix_kernel, sent, gu, mats[s][4]))
         held = (x[s], gz, gg, z_all[s], gu)

time: 301 us -> 290 us (0.963)
  blocking collectives: 244 us -> 259 us
  local copies, waits for them, and re-layouts: 16 us -> 2.57 us
  starting transfers between devices: 12.5 us -> 6.41 us
  waiting for transfers between devices: 8.21 us -> 4.96 us
    all_to_all x13 -> x14, blocking collectives: 200 us -> 216 us  [swap(): return lax.all_to_all(block, ('y', 'z'), 0, 0, tiled=True)]
    unnamed x78 -> x4, local copies, waits for them, and re-layouts: 13.4 us -> 0.01 us
    all_to_all x1 -> x0, waiting for transfers between devices: 5.04 us -> none  [swap(): return lax.all_to_all(block, ('y', 'z'), 0, 0, tiled=True)]
    all_to_all x1 -> x0, starting transfers between devices: 4.6 us -> none  [swap(): return lax.all_to_all(block, ('y', 'z'), 0, 0, tiled=True)]
    pallas_call x14 -> x13, Pallas kernels: 6.58 us -> 5.34 us  [run(): pl.pallas_call(kernel, out_shape=outs, compiler_params=params, cost_estim...]
  transfers between devices with their start and end apart: 7 -> 6, of which waited for: 2 -> 2; matrix products, arithmetic and copies ran while one was open for 1% -> 1% of each run, Pallas kernels for 2% -> 1%
where the time goes in v2:
time: 290 us; the launch traced here: 289 us
  blocking collectives  259 us (89%)
  Pallas kernels  13.4 us (5%)
  starting transfers between devices  6.41 us (2%)
  waiting for transfers between devices  4.96 us (2%)
    all_to_all x14, blocking collectives, swap(): return lax.all_to_all(block, ('y', 'z'), 0, 0, tiled=True)  216 us
    all_to_all x1, blocking collectives, program(): lax.all_to_all(parts.reshape(sections * 2, tokens + 320, 128), ('x', 'c')...  43.5 us
  transfers between devices with their start and end apart: 6, of which 2 were waited for; matrix products, arithmetic and copies ran while one was open for 1% of the time, Pallas kernels for 1%

profile of v2, /device:TPU:1, one launch (start us, length us, event | category | flops | bytes accessed | tf_op | source)
XLA Modules:
  0.0 289.2 jit_solution(7343738875704918364)
XLA Ops:
  0.6 0.7 slice_bitcast_fusion.1
  1.4 0.9 maximum_maximum_fusion.refs_0_
  2.2 3.3 %collective-permute-start.3 = (bf16[320,128]{1,0:T(8,128)(2,1)S(1)}, bf16[320,128]{1,0:T(8,128)(2,1)S(1)}, u32[]{:S(2)}, u32[]{:S(2)}) collective-permute-start(bf16[320,128]{1,0:T(8,128)(2,1)S(1)} %maximum_maximum_fusion.refs_0_), channel_id=1, source_target_pairs={{0,192},{64,0},{128,64},{192,128},{1,193},{65,1},{129,65},{193,129... | collective-permute-start | bytes 245768 | tf_op jit(solution)/shard_map/ppermute | solution.py:296
  5.6 0.5 collective-permute-start.2
  6.1 0.6 collective-permute-start.1
  6.7 0.9 fusion
  7.5 0.0 collective-permute-done.3.refs_3_
  7.5 2.9 collective-permute-done.2.refs_2_
  10.4 2.1 collective-permute-done.1.refs_1_
  12.5 1.3 collective-permute-start.4
  13.8 0.9 constant_dynamic-slice_fusion
  14.7 0.1 collective-permute-start.5
  14.8 0.9 constant_dynamic-slice_fusion.1
  15.7 0.6 collective-permute-start
  16.3 0.1 pad_add_fusion.at_ref
  16.4 0.0 copy-start.1
  16.4 0.0 collective-permute-done.4.refs_4_
  16.4 2.5 shard_map.84
  18.9 0.0 collective-permute-done.other_ref
  18.9 0.0 copy-done.1
  18.9 1.0 shard_map.85
  19.9 0.0 collective-permute-done.5.other_ref
  19.9 21.3 %all_to_all.75.z_ref = bf16[32,8,512]{2,1,0:T(8,128)(2,1)S(1)} all-to-all(bf16[32,8,512]{2,1,0:T(8,128)(2,1)S(1)} %get-tuple-element.62), channel_id=1, replica_groups=mesh['x'=4,'y'=4,'z'=8,'c'=2] {'y','z'}, dimensions={0} | all-to-all | bytes 524288 | tf_op jit(solution)/shard_map/all_to_all | solution.py:310
  41.2 0.2 shard_map.86
  41.5 15.9 %all_to_all.76.u_ref = bf16[32,8,512]{2,1,0:T(8,128)(2,1)S(1)} all-to-all(bf16[32,8,512]{2,1,0:T(8,128)(2,1)S(1)} %shard_map.86), channel_id=1, replica_groups=mesh['x'=4,'y'=4,'z'=8,'c'=2] {'y','z'}, dimensions={0} | all-to-all | bytes 524288 | tf_op jit(solution)/shard_map/all_to_all | solution.py:310
  57.3 0.5 shard_map.87
  57.8 15.6 %all_to_all.77.z_ref = bf16[32,8,512]{2,1,0:T(8,128)(2,1)S(1)} all-to-all(bf16[32,8,512]{2,1,0:T(8,128)(2,1)S(1)} %get-tuple-element.67), channel_id=1, replica_groups=mesh['x'=4,'y'=4,'z'=8,'c'=2] {'y','z'}, dimensions={0} | all-to-all | bytes 524288 | tf_op jit(solution)/shard_map/all_to_all | solution.py:310
  73.4 0.0 copy-start
  73.4 0.2 shard_map.88
  73.7 15.1 %all_to_all.78.u_ref = bf16[32,8,512]{2,1,0:T(8,128)(2,1)S(1)} all-to-all(bf16[32,8,512]{2,1,0:T(8,128)(2,1)S(1)} %shard_map.88), channel_id=1, replica_groups=mesh['x'=4,'y'=4,'z'=8,'c'=2] {'y','z'}, dimensions={0} | all-to-all | bytes 524288 | tf_op jit(solution)/shard_map/all_to_all | solution.py:310
  88.7 0.5 shard_map.89
  89.2 14.2 %all_to_all.79.z_ref = bf16[32,8,512]{2,1,0:T(8,128)(2,1)S(1)} all-to-all(bf16[32,8,512]{2,1,0:T(8,128)(2,1)S(1)} %get-tuple-element.72), channel_id=1, replica_groups=mesh['x'=4,'y'=4,'z'=8,'c'=2] {'y','z'}, dimensions={0} | all-to-all | bytes 524288 | tf_op jit(solution)/shard_map/all_to_all | solution.py:310
  103.4 0.2 shard_map.90
  103.7 14.0 %all_to_all.80.u_ref = bf16[32,8,512]{2,1,0:T(8,128)(2,1)S(1)} all-to-all(bf16[32,8,512]{2,1,0:T(8,128)(2,1)S(1)} %shard_map.90), channel_id=1, replica_groups=mesh['x'=4,'y'=4,'z'=8,'c'=2] {'y','z'}, dimensions={0} | all-to-all | bytes 524288 | tf_op jit(solution)/shard_map/all_to_all | solution.py:310
  117.7 0.0 copy-done
  117.7 1.3 shard_map.91
  118.9 15.6 %all_to_all.81.pair_ref.took_ref = bf16[32,16,512]{2,1,0:T(8,128)(2,1)S(1)} all-to-all(bf16[32,16,512]{2,1,0:T(8,128)(2,1)S(1)} %get-tuple-element.79), channel_id=1, replica_groups=mesh['x'=4,'y'=4,'z'=8,'c'=2] {'y','z'}, dimensions={0} | all-to-all | bytes 1048576 | tf_op jit(solution)/shard_map/all_to_all | solution.py:310
  134.6 0.3 shard_map.92
  134.9 16.8 %all_to_all.82.pair_ref.gave_ref = bf16[32,16,512]{2,1,0:T(8,128)(2,1)S(1)} all-to-all(bf16[32,16,512]{2,1,0:T(8,128)(2,1)S(1)} %shard_map.92), channel_id=1, replica_groups=mesh['x'=4,'y'=4,'z'=8,'c'=2] {'y','z'}, dimensions={0} | all-to-all | bytes 1048576 | tf_op jit(solution)/shard_map/all_to_all | solution.py:310
  151.7 0.7 shard_map.93
  152.4 0.8 shard_map.94.held_ref
  153.2 14.9 %all_to_all.83.z_ref.gu_ref = bf16[32,8,512]{2,1,0:T(8,128)(2,1)S(1)} all-to-all(bf16[32,8,512]{2,1,0:T(8,128)(2,1)S(1)} %get-tuple-element.88), channel_id=1, replica_groups=mesh['x'=4,'y'=4,'z'=8,'c'=2] {'y','z'}, dimensions={0} | all-to-all | bytes 524288 | tf_op jit(solution)/shard_map/all_to_all | solution.py:310
  168.1 0.2 shard_map.95
  168.4 13.9 %all_to_all.84.gz_ref = bf16[32,8,512]{2,1,0:T(8,128)(2,1)S(1)} all-to-all(bf16[32,8,512]{2,1,0:T(8,128)(2,1)S(1)} %shard_map.95), channel_id=1, replica_groups=mesh['x'=4,'y'=4,'z'=8,'c'=2] {'y','z'}, dimensions={0} | all-to-all | bytes 524288 | tf_op jit(solution)/shard_map/all_to_all | solution.py:310
  182.3 0.5 shard_map.96
  182.8 0.8 shard_map.97.held_ref
  183.6 13.9 %all_to_all.85.z_ref.gu_ref = bf16[32,8,512]{2,1,0:T(8,128)(2,1)S(1)} all-to-all(bf16[32,8,512]{2,1,0:T(8,128)(2,1)S(1)} %get-tuple-element.96), channel_id=1, replica_groups=mesh['x'=4,'y'=4,'z'=8,'c'=2] {'y','z'}, dimensions={0} | all-to-all | bytes 524288 | tf_op jit(solution)/shard_map/all_to_all | solution.py:310
  197.5 0.2 shard_map.98
  197.7 15.0 %all_to_all.86.gz_ref = bf16[32,8,512]{2,1,0:T(8,128)(2,1)S(1)} all-to-all(bf16[32,8,512]{2,1,0:T(8,128)(2,1)S(1)} %shard_map.98), channel_id=1, replica_groups=mesh['x'=4,'y'=4,'z'=8,'c'=2] {'y','z'}, dimensions={0} | all-to-all | bytes 524288 | tf_op jit(solution)/shard_map/all_to_all | solution.py:310
  212.7 0.5 shard_map.99
  213.2 0.8 shard_map.100.held_ref
  214.0 15.6 %all_to_all.87.z_ref.gu_ref = bf16[32,8,512]{2,1,0:T(8,128)(2,1)S(1)} all-to-all(bf16[32,8,512]{2,1,0:T(8,128)(2,1)S(1)} %get-tuple-element.104), channel_id=1, replica_groups=mesh['x'=4,'y'=4,'z'=8,'c'=2] {'y','z'}, dimensions={0} | all-to-all | bytes 524288 | tf_op jit(solution)/shard_map/all_to_all | solution.py:310
  229.6 0.2 shard_map.101
  229.9 13.8 %all_to_all.88.gz_ref = bf16[32,8,512]{2,1,0:T(8,128)(2,1)S(1)} all-to-all(bf16[32,8,512]{2,1,0:T(8,128)(2,1)S(1)} %shard_map.101), channel_id=1, replica_groups=mesh['x'=4,'y'=4,'z'=8,'c'=2] {'y','z'}, dimensions={0} | all-to-all | bytes 524288 | tf_op jit(solution)/shard_map/all_to_all | solution.py:310
  243.7 0.9 shard_map.102
  244.6 43.5 %all_to_all.89.got_ref = bf16[8,832,128]{2,1,0:T(8,128)(2,1)S(1)} all-to-all(bf16[8,832,128]{2,1,0:T(8,128)(2,1)S(1)} %bitcast.19), channel_id=1, replica_groups=mesh['x'=4,'y'=4,'z'=8,'c'=2] {'x','c'}, dimensions={0} | all-to-all | bytes 3407872 | tf_op jit(solution)/shard_map/all_to_all | solution.py:403
  288.1 1.1 shard_map.103
  (1 shorter events, 0.0 us)
Async XLA Ops:
  2.2 5.3 %collective-permute-start.3 = (bf16[320,128]{1,0:T(8,128)(2,1)S(1)}, bf16[320,128]{1,0:T(8,128)(2,1)S(1)}, u32[]{:S(2)}, u32[]{:S(2)}) collective-permute-start(bf16[320,128]{1,0:T(8,128)(2,1)S(1)} %maximum_maximum_fusion.refs_0_), channel_id=1, source_target_pairs={{0,192},{64,0},{128,64},{192,128},{1,193},{65,1},{129,65},{193,129... | collective-permute-start | bytes 245768 | tf_op jit(solution)/shard_map/ppermute | solution.py:296
  5.6 4.9 %collective-permute-start.2 = (bf16[320,128]{1,0:T(8,128)(2,1)S(1)}, bf16[320,128]{1,0:T(8,128)(2,1)S(1)}, u32[]{:S(2)}, u32[]{:S(2)}) collective-permute-start(bf16[320,128]{1,0:T(8,128)(2,1)S(1)} %maximum_maximum_fusion.refs_0_), channel_id=1, source_target_pairs={{0,128},{64,192},{128,0},{192,64},{1,129},{65,193},{129,1},{193,65... | collective-permute-start | bytes 245768 | tf_op jit(solution)/shard_map/ppermute | solution.py:296
  6.1 6.4 %collective-permute-start.1 = (bf16[320,128]{1,0:T(8,128)(2,1)S(1)}, bf16[320,128]{1,0:T(8,128)(2,1)S(1)}, u32[]{:S(2)}, u32[]{:S(2)}) collective-permute-start(bf16[320,128]{1,0:T(8,128)(2,1)S(1)} %maximum_maximum_fusion.refs_0_), channel_id=1, source_target_pairs={{0,64},{64,128},{128,192},{192,0},{1,65},{65,129},{129,193},{193,1... | collective-permute-start | bytes 245768 | tf_op jit(solution)/shard_map/ppermute | solution.py:296
  12.5 3.9 %collective-permute-start.4 = (bf16[4,320,128]{2,1,0:T(8,128)(2,1)S(1)}, bf16[4,320,128]{2,1,0:T(8,128)(2,1)S(1)}, u32[]{:S(2)}, u32[]{:S(2)}) collective-permute-start(bf16[4,320,128]{2,1,0:T(8,128)(2,1)S(1)} %pad_maximum_fusion), channel_id=1, source_target_pairs={{0,1},{1,0},{2,3},{3,2},{4,5},{5,4},{6,7},{7,6},{8,9},{9,8},{10,11... | collective-permute-start | bytes 983048 | tf_op jit(solution)/shard_map/ppermute | solution.py:293
  14.7 5.2 %collective-permute-start.5 = (bf16[512,128]{1,0:T(8,128)(2,1)S(1)}, bf16[512,128]{1,0:T(8,128)(2,1)S(1)}, u32[]{:S(2)}, u32[]{:S(2)}) collective-permute-start(bf16[512,128]{1,0:T(8,128)(2,1)S(1)} %constant_dynamic-slice_fusion), channel_id=1, source_target_pairs={{0,1},{1,0},{2,3},{3,2},{4,5},{5,4},{6,7},{7,6},{8,9},{9,8},{10,11... | collective-permute-start | bytes 393224 | tf_op jit(solution)/shard_map/ppermute | solution.py:293
  15.7 3.1 %collective-permute-start = (bf16[512,128]{1,0:T(8,128)(2,1)S(1)}, bf16[512,128]{1,0:T(8,128)(2,1)S(1)}, u32[]{:S(2)}, u32[]{:S(2)}) collective-permute-start(bf16[512,128]{1,0:T(8,128)(2,1)S(1)} %constant_dynamic-slice_fusion.1), channel_id=1, source_target_pairs={{0,1},{1,0},{2,3},{3,2},{4,5},{5,4},{6,7},{7,6},{8,9},{9,8},{10,11... | collective-permute-start | bytes 393224 | tf_op jit(solution)/shard_map/ppermute | solution.py:293
  16.4 2.5 copy-start.1
  73.4 44.2 %copy-start = (bf16[4096,128]{1,0:T(8,128)(2,1)S(1)}, bf16[4096,128]{1,0:T(8,128)(2,1)}, u32[]{:S(2)}) copy-start(bf16[4096,128]{1,0:T(8,128)(2,1)} %mine_ref.3) | copy-start | bytes 3145732

commit v3 on v2

--- a/solution.py
+++ b/solution.py
@@ -49,39 +49,44 @@
     return jnp.where(core == c, mine, other)
 
 
-def prepare_kernel(at_ref, *refs):
-    shifted, other_ref = refs[:4], refs[4]
-    outs, own_ref = refs[5:-1], refs[-1]
+def pack_kernel(r_ref, g_ref, l_ref, out_ref, pair_ref, sems):
+    copies = [
+        pltpu.make_async_copy(r_ref.at[0, 0], out_ref.at[pl.ds(0, 128)], sems.at[0]),
+        pltpu.make_async_copy(g_ref.at[0, 0], out_ref.at[pl.ds(128, 128)], sems.at[1]),
+        pltpu.make_async_copy(l_ref.at[0], pair_ref, sems.at[2]),
+    ]
+    for copy in copies:
+        copy.start()
+    for copy in copies:
+        copy.wait()
+    both = [pair_ref[i].astype(F32) for i in range(2)]
+    out_ref[256:320, :] = jnp.concatenate(both, axis=1).astype(BF)
+
+
+def prepare_kernel(at_ref, own_ref, other_ref, *refs):
+    outs, wide_ref = refs[:-1], refs[-1]
     sect, core = at_ref[0], at_ref[1]
-    for k in range(4):
-        own_ref[k] = shifted[k][...]
     p = feature_order(256, 256)
     q = position_order(256, 256)
     lane = lax.broadcasted_iota(jnp.int32, (64, 128), 1)
+    wide_ref[...] = jnp.zeros_like(wide_ref)
     for layer in range(4):
-        k = lax.rem(sect - layer + 4, 4)
-        r_out, rt_out, g_out, gt_out, l_out, lt_out = outs[6 * layer : 6 * layer + 6]
-        for start, plain, flipped in ((0, r_out, rt_out), (128, g_out, gt_out)):
-            blocks = [
-                block_of(own_ref, other_ref, c, core, k, start, start + 128).astype(BF)
-                for c in range(2)
-            ]
-            parts = [p[:, 128 * c : 128 * c + 128] for c in range(2)]
-            left = jnp.concatenate([nn(parts[c], blocks[c]) for c in range(2)], axis=1).astype(BF)
-            plain[...] = nt(left, p).astype(BF)
-            left = jnp.concatenate([nt(parts[c], blocks[c]) for c in range(2)], axis=1).astype(BF)
-            flipped[...] = nt(left, p).astype(BF)
-        pairs = []
-        for c in range(2):
-            packed = block_of(own_ref, other_ref, c, core, k, 256, 320)
-            low = jnp.where(lane < 64, packed, 0.0)
-            high = jnp.where(lane < 64, 0.0, packed)
-            pairs.append(jnp.concatenate([low, high], axis=0).astype(BF))
-        parts = [q[:, 128 * c : 128 * c + 128] for c in range(2)]
-        left = jnp.concatenate([nn(parts[c], pairs[c]) for c in range(2)], axis=1).astype(BF)
-        l_out[...] = nt(left, q).astype(BF)
-        left = jnp.concatenate([nt(parts[c], pairs[c]) for c in range(2)], axis=1).astype(BF)
-        lt_out[...] = nt(left, q).astype(BF)
+        apart = layer ^ sect
+        k = apart ^ (apart >> 1)
+        outs_of = outs[6 * layer : 6 * layer + 6]
+        for i, start in enumerate((0, 128, 256)):
+            order = p if i < 2 else q
+            for c in range(2):
+                block = block_of(own_ref, other_ref, c, core, k, start, min(start + 128, 320))
+                if i == 2:
+                    low = jnp.where(lane < 64, block, 0.0)
+                    high = jnp.where(lane < 64, 0.0, block)
+                    block = jnp.concatenate([low, high], axis=0)
+                at = slice(128 * c, 128 * c + 128)
+                wide_ref[i, at, at] = block.astype(BF)
+            wide = wide_ref[i]
+            outs_of[2 * i][...] = nt(nn(order, wide).astype(BF), order).astype(BF)
+            outs_of[2 * i + 1][...] = nt(nt(order, wide).astype(BF), order).astype(BF)
 
 
 def turned(core, mine_ref, other_ref):
@@ -90,10 +95,12 @@
     return (nt(p, mine_ref[...]) + nt(o, other_ref[...])).astype(BF)
 
 
-def first_kernel(at_ref, mine_ref, other_ref, rt_ref, x_ref, z_ref):
-    x = turned(at_ref[1], mine_ref, other_ref)
-    x_ref[...] = x
-    put_rows(z_ref, nn(rt_ref[...], x))
+def turn_kernel(at_ref, mine_ref, other_ref, x_ref):
+    x_ref[...] = turned(at_ref[1], mine_ref, other_ref)
+
+
+def first_kernel(x_ref, rt_ref, z_ref):
+    put_rows(z_ref, nn(rt_ref[...], x_ref[...]))
 
 
 def mix_kernel(z_ref, w_ref, u_ref):
@@ -292,15 +299,19 @@
     def to_other(value):
         return lax.ppermute(value, "c", [(0, 1), (1, 0)])
 
-    def shift(value, k):
-        return lax.ppermute(value, "x", [(i, (i + k) % sections) for i in range(sections)])
-
-    l_flat = jnp.concatenate([l_weight[0, 0], l_weight[0, 1]], axis=1)
-    packed = jnp.concatenate([r_weight[0, 0], g_weight[0, 0], l_flat], axis=0)
-    own = [packed]
-    for k in range(1, sections):
-        own.append(shift(packed, k))
-    other = to_other(jnp.stack(own))
+    packed = pl.pallas_call(
+        pack_kernel,
+        out_shape=sds(320, 128),
+        in_specs=[pl.BlockSpec(memory_space=pltpu.HBM)] * 3,
+        out_specs=pl.BlockSpec(memory_space=pltpu.VMEM),
+        scratch_shapes=[pltpu.VMEM((2, 64, 64), BF), pltpu.SemaphoreType.DMA((3,))],
+        compiler_params=pltpu.CompilerParams(vmem_limit_bytes=67043328),
+    )(r_weight, g_weight, l_weight)
+    own = packed[None]
+    for bit in (1, 3):
+        arrived = lax.ppermute(own, "x", [(i, i ^ bit) for i in range(sections)])
+        own = jnp.concatenate([own, arrived])
+    other = to_other(own)
 
     def sent_over(whole):
         start = (sect * 2 + 1 - core) * tokens
@@ -315,23 +326,16 @@
     outs = run(
         prepare_kernel,
         [sds(256, 256)] * 24,
-        *own,
+        own,
         other,
         at=at,
         dots=24,
-        scratch=[pltpu.VMEM((4, 320, 128), BF)],
+        scratch=[pltpu.VMEM((3, 256, 256), BF)],
     )
     mats = [outs[6 * s : 6 * s + 6] for s in range(sections)]
-    x0, z = run(
-        first_kernel,
-        [flat, sent],
-        inputs,
-        sent_over(inputs),
-        mats[0][1],
-        at=at,
-        dots=2,
-        blocks=[mine, None, None],
-    )
+    from_other = sent_over(inputs)
+    x0 = run(turn_kernel, flat, inputs, from_other, at=at, blocks=[mine, None])
+    z = run(first_kernel, sent, x0, mats[0][1])
     crossed = sent_over(cotangent)
     z, crossed = lax.optimization_barrier((z, crossed))
     x = [x0]

time: 290 us -> 295 us (1.017)
  starting transfers between devices: 6.41 us -> 10.6 us
    ppermute x3, starting transfers between devices: 1.96 us -> 5.64 us  [to_other(): return lax.ppermute(value, 'c', [(0, 1), (1, 0)])]
  transfers between devices with their start and end apart: 6 -> 5, of which waited for: 2 -> 2; matrix products, arithmetic and copies ran while one was open for 1% -> 1% of each run, Pallas kernels for 1% -> 1%
where the time goes in v3:
time: 295 us; the launch traced here: 294 us
  blocking collectives  259 us (88%)
  Pallas kernels  15.1 us (5%)
  starting transfers between devices  10.6 us (4%)
  waiting for transfers between devices  4.76 us (2%)
    all_to_all x14, blocking collectives, swap(): return lax.all_to_all(block, ('y', 'z'), 0, 0, tiled=True)  214 us
    all_to_all x1, blocking collectives, program(): lax.all_to_all(parts.reshape(sections * 2, tokens + 320, 128), ('x', 'c')...  44.9 us
  transfers between devices with their start and end apart: 5, of which 2 were waited for; matrix products, arithmetic and copies ran while one was open for 1% of the time, Pallas kernels for 1%

profile of v3, /device:TPU:1, one launch (start us, length us, event | category | flops | bytes accessed | tf_op | source)
XLA Modules:
  0.0 293.9 jit_solution(18088246711760575666)
XLA Ops:
  0.6 1.5 shard_map.85
  2.2 0.0 copy-start.1
  2.2 2.1 collective-permute-start.1
  4.3 2.0 collective-permute-done.1
  6.3 0.9 pad_maximum_fusion.1
  7.2 2.8 collective-permute-start.2
  10.1 2.7 collective-permute-done.2
  12.8 0.9 pad_maximum_fusion.own_ref
  13.7 5.0 %collective-permute-start.3 = (bf16[4,320,128]{2,1,0:T(8,128)(2,1)S(1)}, bf16[4,320,128]{2,1,0:T(8,128)(2,1)S(1)}, u32[]{:S(2)}, u32[]{:S(2)}) collective-permute-start(bf16[4,320,128]{2,1,0:T(8,128)(2,1)S(1)} %pad_maximum_fusion.own_ref), channel_id=1, source_target_pairs={{0,1},{1,0},{2,3},{3,2},{4,5},{5,4},{6,7},{7,6},{8,9},{9,8},{10,11... | collective-permute-start | bytes 983048 | tf_op jit(solution)/shard_map/ppermute | solution.py:300
  18.6 0.9 constant_dynamic-slice_fusion.1
  19.6 0.1 collective-permute-start
  19.7 0.9 constant_dynamic-slice_fusion
  20.6 0.6 collective-permute-start.4
  21.2 0.1 pad_add_fusion.at_ref
  21.2 0.0 collective-permute-done.other_ref
  21.2 0.0 copy-done.1
  21.2 0.8 shard_map.84.x_ref
  22.1 0.0 collective-permute-done.3.other_ref
  22.1 2.6 shard_map.86
  24.7 0.2 shard_map.87
  24.9 0.0 collective-permute-done.4.other_ref
  24.9 19.6 %all_to_all.75.z_ref = bf16[32,8,512]{2,1,0:T(8,128)(2,1)S(1)} all-to-all(bf16[32,8,512]{2,1,0:T(8,128)(2,1)S(1)} %shard_map.87), channel_id=1, replica_groups=mesh['x'=4,'y'=4,'z'=8,'c'=2] {'y','z'}, dimensions={0} | all-to-all | bytes 524288 | tf_op jit(solution)/shard_map/all_to_all | solution.py:321
  44.5 0.2 shard_map.88
  44.8 15.9 %all_to_all.76.u_ref = bf16[32,8,512]{2,1,0:T(8,128)(2,1)S(1)} all-to-all(bf16[32,8,512]{2,1,0:T(8,128)(2,1)S(1)} %shard_map.88), channel_id=1, replica_groups=mesh['x'=4,'y'=4,'z'=8,'c'=2] {'y','z'}, dimensions={0} | all-to-all | bytes 524288 | tf_op jit(solution)/shard_map/all_to_all | solution.py:321
  60.6 0.5 shard_map.89
  61.1 15.6 %all_to_all.77.z_ref = bf16[32,8,512]{2,1,0:T(8,128)(2,1)S(1)} all-to-all(bf16[32,8,512]{2,1,0:T(8,128)(2,1)S(1)} %get-tuple-element.63), channel_id=1, replica_groups=mesh['x'=4,'y'=4,'z'=8,'c'=2] {'y','z'}, dimensions={0} | all-to-all | bytes 524288 | tf_op jit(solution)/shard_map/all_to_all | solution.py:321
  76.7 0.0 copy-start
  76.7 0.2 shard_map.90
  77.0 15.1 %all_to_all.78.u_ref = bf16[32,8,512]{2,1,0:T(8,128)(2,1)S(1)} all-to-all(bf16[32,8,512]{2,1,0:T(8,128)(2,1)S(1)} %shard_map.90), channel_id=1, replica_groups=mesh['x'=4,'y'=4,'z'=8,'c'=2] {'y','z'}, dimensions={0} | all-to-all | bytes 524288 | tf_op jit(solution)/shard_map/all_to_all | solution.py:321
  92.0 0.5 shard_map.91
  92.5 14.2 %all_to_all.79.z_ref = bf16[32,8,512]{2,1,0:T(8,128)(2,1)S(1)} all-to-all(bf16[32,8,512]{2,1,0:T(8,128)(2,1)S(1)} %get-tuple-element.68), channel_id=1, replica_groups=mesh['x'=4,'y'=4,'z'=8,'c'=2] {'y','z'}, dimensions={0} | all-to-all | bytes 524288 | tf_op jit(solution)/shard_map/all_to_all | solution.py:321
  106.7 0.2 shard_map.92
  107.0 14.0 %all_to_all.80.u_ref = bf16[32,8,512]{2,1,0:T(8,128)(2,1)S(1)} all-to-all(bf16[32,8,512]{2,1,0:T(8,128)(2,1)S(1)} %shard_map.92), channel_id=1, replica_groups=mesh['x'=4,'y'=4,'z'=8,'c'=2] {'y','z'}, dimensions={0} | all-to-all | bytes 524288 | tf_op jit(solution)/shard_map/all_to_all | solution.py:321
  121.0 0.0 copy-done
  121.0 1.3 shard_map.93
  122.2 15.6 %all_to_all.81.pair_ref.took_ref = bf16[32,16,512]{2,1,0:T(8,128)(2,1)S(1)} all-to-all(bf16[32,16,512]{2,1,0:T(8,128)(2,1)S(1)} %get-tuple-element.75), channel_id=1, replica_groups=mesh['x'=4,'y'=4,'z'=8,'c'=2] {'y','z'}, dimensions={0} | all-to-all | bytes 1048576 | tf_op jit(solution)/shard_map/all_to_all | solution.py:321
  137.9 0.3 shard_map.94
  138.2 16.8 %all_to_all.82.pair_ref.gave_ref = bf16[32,16,512]{2,1,0:T(8,128)(2,1)S(1)} all-to-all(bf16[32,16,512]{2,1,0:T(8,128)(2,1)S(1)} %shard_map.94), channel_id=1, replica_groups=mesh['x'=4,'y'=4,'z'=8,'c'=2] {'y','z'}, dimensions={0} | all-to-all | bytes 1048576 | tf_op jit(solution)/shard_map/all_to_all | solution.py:321
  155.0 0.7 shard_map.95
  155.7 0.8 shard_map.96.held_ref
  156.5 14.9 %all_to_all.83.z_ref.gu_ref = bf16[32,8,512]{2,1,0:T(8,128)(2,1)S(1)} all-to-all(bf16[32,8,512]{2,1,0:T(8,128)(2,1)S(1)} %get-tuple-element.84), channel_id=1, replica_groups=mesh['x'=4,'y'=4,'z'=8,'c'=2] {'y','z'}, dimensions={0} | all-to-all | bytes 524288 | tf_op jit(solution)/shard_map/all_to_all | solution.py:321
  171.4 0.2 shard_map.97
  171.6 13.9 %all_to_all.84.gz_ref = bf16[32,8,512]{2,1,0:T(8,128)(2,1)S(1)} all-to-all(bf16[32,8,512]{2,1,0:T(8,128)(2,1)S(1)} %shard_map.97), channel_id=1, replica_groups=mesh['x'=4,'y'=4,'z'=8,'c'=2] {'y','z'}, dimensions={0} | all-to-all | bytes 524288 | tf_op jit(solution)/shard_map/all_to_all | solution.py:321
  185.6 0.5 shard_map.98
  186.0 0.8 shard_map.99.held_ref
  186.8 13.9 %all_to_all.85.z_ref.gu_ref = bf16[32,8,512]{2,1,0:T(8,128)(2,1)S(1)} all-to-all(bf16[32,8,512]{2,1,0:T(8,128)(2,1)S(1)} %get-tuple-element.92), channel_id=1, replica_groups=mesh['x'=4,'y'=4,'z'=8,'c'=2] {'y','z'}, dimensions={0} | all-to-all | bytes 524288 | tf_op jit(solution)/shard_map/all_to_all | solution.py:321
  200.7 0.2 shard_map.100
  201.0 15.1 %all_to_all.86.gz_ref = bf16[32,8,512]{2,1,0:T(8,128)(2,1)S(1)} all-to-all(bf16[32,8,512]{2,1,0:T(8,128)(2,1)S(1)} %shard_map.100), channel_id=1, replica_groups=mesh['x'=4,'y'=4,'z'=8,'c'=2] {'y','z'}, dimensions={0} | all-to-all | bytes 524288 | tf_op jit(solution)/shard_map/all_to_all | solution.py:321
  216.0 0.5 shard_map.101
  216.5 0.8 shard_map.102.held_ref
  217.3 15.6 %all_to_all.87.z_ref.gu_ref = bf16[32,8,512]{2,1,0:T(8,128)(2,1)S(1)} all-to-all(bf16[32,8,512]{2,1,0:T(8,128)(2,1)S(1)} %get-tuple-element.100), channel_id=1, replica_groups=mesh['x'=4,'y'=4,'z'=8,'c'=2] {'y','z'}, dimensions={0} | all-to-all | bytes 524288 | tf_op jit(solution)/shard_map/all_to_all | solution.py:321
  232.9 0.2 shard_map.103
  233.1 13.8 %all_to_all.88.gz_ref = bf16[32,8,512]{2,1,0:T(8,128)(2,1)S(1)} all-to-all(bf16[32,8,512]{2,1,0:T(8,128)(2,1)S(1)} %shard_map.103), channel_id=1, replica_groups=mesh['x'=4,'y'=4,'z'=8,'c'=2] {'y','z'}, dimensions={0} | all-to-all | bytes 524288 | tf_op jit(solution)/shard_map/all_to_all | solution.py:321
  246.9 0.9 shard_map.104
  247.9 44.9 %all_to_all.89.got_ref = bf16[8,832,128]{2,1,0:T(8,128)(2,1)S(1)} all-to-all(bf16[8,832,128]{2,1,0:T(8,128)(2,1)S(1)} %bitcast.9), channel_id=1, replica_groups=mesh['x'=4,'y'=4,'z'=8,'c'=2] {'x','c'}, dimensions={0} | all-to-all | bytes 3407872 | tf_op jit(solution)/shard_map/all_to_all | solution.py:407
  292.8 1.1 shard_map.105
Async XLA Ops:
  2.2 19.1 %copy-start.1 = (bf16[4096,128]{1,0:T(8,128)(2,1)S(1)}, bf16[4096,128]{1,0:T(8,128)(2,1)}, u32[]{:S(2)}) copy-start(bf16[4096,128]{1,0:T(8,128)(2,1)} %mine_ref.2) | copy-start | bytes 3145732
  2.2 4.2 %collective-permute-start.1 = (bf16[1,320,128]{2,1,0:T(8,128)(2,1)}, bf16[1,320,128]{2,1,0:T(8,128)(2,1)S(1)}, u32[]{:S(2)}, u32[]{:S(2)}) collective-permute-start(bf16[1,320,128]{2,1,0:T(8,128)(2,1)} %bitcast.10), channel_id=1, source_target_pairs={{0,64},{64,0},{128,192},{192,128},{1,65},{65,1},{129,193},{193,129... | collective-permute-start | bytes 245768 | tf_op jit(solution)/shard_map/ppermute | solution.py:312
  7.2 5.5 %collective-permute-start.2 = (bf16[2,320,128]{2,1,0:T(8,128)(2,1)S(1)}, bf16[2,320,128]{2,1,0:T(8,128)(2,1)S(1)}, u32[]{:S(2)}, u32[]{:S(2)}) collective-permute-start(bf16[2,320,128]{2,1,0:T(8,128)(2,1)S(1)} %pad_maximum_fusion.1), channel_id=1, source_target_pairs={{0,192},{64,128},{128,64},{192,0},{1,193},{65,129},{129,65},{193,1... | collective-permute-start | bytes 491528 | tf_op jit(solution)/shard_map/ppermute | solution.py:312
  13.7 8.4 %collective-permute-start.3 = (bf16[4,320,128]{2,1,0:T(8,128)(2,1)S(1)}, bf16[4,320,128]{2,1,0:T(8,128)(2,1)S(1)}, u32[]{:S(2)}, u32[]{:S(2)}) collective-permute-start(bf16[4,320,128]{2,1,0:T(8,128)(2,1)S(1)} %pad_maximum_fusion.own_ref), channel_id=1, source_target_pairs={{0,1},{1,0},{2,3},{3,2},{4,5},{5,4},{6,7},{7,6},{8,9},{9,8},{10,11... | collective-permute-start | bytes 983048 | tf_op jit(solution)/shard_map/ppermute | solution.py:300
  19.6 1.7 collective-permute-start
  20.6 4.3 %collective-permute-start.4 = (bf16[512,128]{1,0:T(8,128)(2,1)S(1)}, bf16[512,128]{1,0:T(8,128)(2,1)S(1)}, u32[]{:S(2)}, u32[]{:S(2)}) collective-permute-start(bf16[512,128]{1,0:T(8,128)(2,1)S(1)} %constant_dynamic-slice_fusion), channel_id=1, source_target_pairs={{0,1},{1,0},{2,3},{3,2},{4,5},{5,4},{6,7},{7,6},{8,9},{9,8},{10,11... | collective-permute-start | bytes 393224 | tf_op jit(solution)/shard_map/ppermute | solution.py:300
  76.7 44.2 %copy-start = (bf16[4096,128]{1,0:T(8,128)(2,1)S(1)}, bf16[4096,128]{1,0:T(8,128)(2,1)}, u32[]{:S(2)}) copy-start(bf16[4096,128]{1,0:T(8,128)(2,1)} %mine_ref.3) | copy-start | bytes 3145732

commit v4 on v2

--- a/solution.py
+++ b/solution.py
@@ -90,10 +90,12 @@
     return (nt(p, mine_ref[...]) + nt(o, other_ref[...])).astype(BF)
 
 
-def first_kernel(at_ref, mine_ref, other_ref, rt_ref, x_ref, z_ref):
-    x = turned(at_ref[1], mine_ref, other_ref)
-    x_ref[...] = x
-    put_rows(z_ref, nn(rt_ref[...], x))
+def turn_kernel(at_ref, mine_ref, other_ref, x_ref):
+    x_ref[...] = turned(at_ref[1], mine_ref, other_ref)
+
+
+def first_kernel(x_ref, rt_ref, z_ref):
+    put_rows(z_ref, nn(rt_ref[...], x_ref[...]))
 
 
 def mix_kernel(z_ref, w_ref, u_ref):
@@ -212,12 +214,21 @@
     put_parts(parts_of(x_ref[...], gz, gg_ref[...], z, gu, lower), out_ref)
 
 
-def settle_kernel(got_ref, y_out, r_out, g_out, l_out):
+def pick_kernel(at_ref, got_ref, out_ref):
+    for i in range(4):
+        out_ref[i] = got_ref[i, 1 - at_ref[1]]
+
+
+def settle_kernel(at_ref, got_ref, other_ref, y_out, r_out, g_out, l_out):
+    core = at_ref[1]
     n = y_out.shape[0] // 8
     total = None
-    for i in range(8):
-        y_out[n * i : n * i + n, :] = got_ref[i, :n, :]
-        part = got_ref[i, n:, :].astype(F32)
+    for i in range(4):
+        here = pl.multiple_of((2 * i + core) * n, n)
+        there = pl.multiple_of((2 * i + 1 - core) * n, n)
+        y_out[pl.ds(here, n), :] = got_ref[i, core, :n, :]
+        y_out[pl.ds(there, n), :] = other_ref[i, :n, :]
+        part = got_ref[i, core, n:, :].astype(F32) + other_ref[i, n:, :].astype(F32)
         total = part if total is None else total + part
     r_out[...] = total[:128]
     g_out[...] = total[128:256]
@@ -322,16 +333,9 @@
         scratch=[pltpu.VMEM((4, 320, 128), BF)],
     )
     mats = [outs[6 * s : 6 * s + 6] for s in range(sections)]
-    x0, z = run(
-        first_kernel,
-        [flat, sent],
-        inputs,
-        sent_over(inputs),
-        mats[0][1],
-        at=at,
-        dots=2,
-        blocks=[mine, None, None],
-    )
+    from_other = sent_over(inputs)
+    x0 = run(turn_kernel, flat, inputs, from_other, at=at, blocks=[mine, None])
+    z = run(first_kernel, sent, x0, mats[0][1])
     crossed = sent_over(cotangent)
     z, crossed = lax.optimization_barrier((z, crossed))
     x = [x0]
@@ -400,9 +404,8 @@
             )
             parts = run_parts(parts_kernel, s, whole, *held, y, parts)
     parts = run_parts(last_kernel, 0, whole, *held, y, mats[0][0], mats[0][2], parts)
-    got = lax.all_to_all(
-        parts.reshape(sections * 2, tokens + 320, 128), ("x", "c"), 0, 0, tiled=True
-    )
+    got = lax.all_to_all(parts, "x", 0, 0, tiled=True)
+    other = to_other(run(pick_kernel, sds(sections, tokens + 320, 128), got, at=at))
     y_out, r_grad, g_grad, l_grad = run(
         settle_kernel,
         [
@@ -412,6 +415,8 @@
             sds(2, 64, 64, dtype=F32),
         ],
         got,
+        other,
+        at=at,
     )
     return y_out[None], r_grad[None, None], g_grad[None, None], l_grad[None]
 

time: 290 us -> 286 us (0.986)
  blocking collectives: 259 us -> 232 us
  starting transfers between devices: 6.41 us -> 26.3 us
    all_to_all x1, blocking collectives: 43.5 us -> 16 us  [program(): got = lax.all_to_all(parts, 'x', 0, 0, tiled=True)]
    ppermute x3 -> x4, starting transfers between devices: 1.96 us -> 21.9 us  [to_other(): return lax.ppermute(value, 'c', [(0, 1), (1, 0)])]
    pallas_call x3 -> x5, Pallas kernels: 4.75 us -> 6.84 us  [run(): pl.pallas_call(kernel, out_shape=outs, grid_spec=pltpu.PrefetchScalarGrid...]
  transfers between devices with their start and end apart: 6 -> 7, of which waited for: 2 -> 3; matrix products, arithmetic and copies ran while one was open for 1% -> 1% of each run, Pallas kernels for 1% -> 1%
where the time goes in v4:
time: 286 us; the launch traced here: 285 us
  blocking collectives  232 us (81%)
  starting transfers between devices  26.3 us (9%)
  Pallas kernels  14.6 us (5%)
  waiting for transfers between devices  6.96 us (2%)
    all_to_all x14, blocking collectives, swap(): return lax.all_to_all(block, ('y', 'z'), 0, 0, tiled=True)  216 us
    ppermute x4, starting transfers between devices, to_other(): return lax.ppermute(value, 'c', [(0, 1), (1, 0)])  21.9 us
    all_to_all x1, blocking collectives, program(): got = lax.all_to_all(parts, 'x', 0, 0, tiled=True)  16 us
    pallas_call x5, Pallas kernels, run(): pl.pallas_call(kernel, out_shape=outs, grid_spec=pltpu.PrefetchScalarGrid...  6.84 us
  transfers between devices with their start and end apart: 7, of which 3 were waited for; matrix products, arithmetic and copies ran while one was open for 1% of the time, Pallas kernels for 1%

profile of v4, /device:TPU:1, one launch (start us, length us, event | category | flops | bytes accessed | tf_op | source)
XLA Modules:
  0.0 285.0 jit_solution(11922266400782535225)
XLA Ops:
  0.6 0.0 copy-start.1
  0.6 0.8 slice_bitcast_fusion.1
  1.5 0.9 maximum_maximum_fusion.refs_0_
  2.3 3.3 %collective-permute-start.3 = (bf16[320,128]{1,0:T(8,128)(2,1)S(1)}, bf16[320,128]{1,0:T(8,128)(2,1)S(1)}, u32[]{:S(2)}, u32[]{:S(2)}) collective-permute-start(bf16[320,128]{1,0:T(8,128)(2,1)S(1)} %maximum_maximum_fusion.refs_0_), channel_id=1, source_target_pairs={{0,192},{64,0},{128,64},{192,128},{1,193},{65,1},{129,65},{193,129... | collective-permute-start | bytes 245768 | tf_op jit(solution)/shard_map/ppermute | solution.py:307
  5.6 0.5 collective-permute-start.2
  6.2 0.6 collective-permute-start.1
  6.8 0.9 fusion
  7.6 0.0 collective-permute-done.3.refs_3_
  7.6 2.9 %collective-permute-done.2.refs_2_ = bf16[320,128]{1,0:T(8,128)(2,1)S(1)} collective-permute-done((bf16[320,128]{1,0:T(8,128)(2,1)S(1)}, bf16[320,128]{1,0:T(8,128)(2,1)S(1)}, u32[]{:S(2)}, u32[]{:S(2)}) %collective-permute-start.2) | collective-permute-done | bytes 81952 | tf_op jit(solution)/shard_map/ppermute | solution.py:307
  10.5 2.1 collective-permute-done.1.refs_1_
  12.6 1.3 collective-permute-start.4
  13.9 0.9 constant_dynamic-slice_fusion.1
  14.8 0.1 collective-permute-start
  14.9 0.9 constant_dynamic-slice_fusion
  15.8 0.6 collective-permute-start.5
  16.4 0.1 pad_add_fusion.at_ref
  16.5 0.0 collective-permute-done.other_ref
  16.5 0.0 copy-done.1
  16.5 0.8 shard_map.84.x_ref
  17.4 0.0 collective-permute-done.4.refs_4_
  17.4 2.5 shard_map.85
  19.9 0.2 shard_map.86
  20.1 0.0 collective-permute-done.5.other_ref
  20.1 21.3 %all_to_all.75.z_ref = bf16[32,8,512]{2,1,0:T(8,128)(2,1)S(1)} all-to-all(bf16[32,8,512]{2,1,0:T(8,128)(2,1)S(1)} %shard_map.86), channel_id=1, replica_groups=mesh['x'=4,'y'=4,'z'=8,'c'=2] {'y','z'}, dimensions={0} | all-to-all | bytes 524288 | tf_op jit(solution)/shard_map/all_to_all | solution.py:321
  41.4 0.2 shard_map.87
  41.6 15.9 %all_to_all.76.u_ref = bf16[32,8,512]{2,1,0:T(8,128)(2,1)S(1)} all-to-all(bf16[32,8,512]{2,1,0:T(8,128)(2,1)S(1)} %shard_map.87), channel_id=1, replica_groups=mesh['x'=4,'y'=4,'z'=8,'c'=2] {'y','z'}, dimensions={0} | all-to-all | bytes 524288 | tf_op jit(solution)/shard_map/all_to_all | solution.py:321
  57.5 0.5 shard_map.88
  58.0 15.6 %all_to_all.77.z_ref = bf16[32,8,512]{2,1,0:T(8,128)(2,1)S(1)} all-to-all(bf16[32,8,512]{2,1,0:T(8,128)(2,1)S(1)} %get-tuple-element.63), channel_id=1, replica_groups=mesh['x'=4,'y'=4,'z'=8,'c'=2] {'y','z'}, dimensions={0} | all-to-all | bytes 524288 | tf_op jit(solution)/shard_map/all_to_all | solution.py:321
  73.6 0.0 copy-start
  73.6 0.2 shard_map.89
  73.8 15.1 %all_to_all.78.u_ref = bf16[32,8,512]{2,1,0:T(8,128)(2,1)S(1)} all-to-all(bf16[32,8,512]{2,1,0:T(8,128)(2,1)S(1)} %shard_map.89), channel_id=1, replica_groups=mesh['x'=4,'y'=4,'z'=8,'c'=2] {'y','z'}, dimensions={0} | all-to-all | bytes 524288 | tf_op jit(solution)/shard_map/all_to_all | solution.py:321
  88.9 0.5 shard_map.90
  89.4 14.2 %all_to_all.79.z_ref = bf16[32,8,512]{2,1,0:T(8,128)(2,1)S(1)} all-to-all(bf16[32,8,512]{2,1,0:T(8,128)(2,1)S(1)} %get-tuple-element.68), channel_id=1, replica_groups=mesh['x'=4,'y'=4,'z'=8,'c'=2] {'y','z'}, dimensions={0} | all-to-all | bytes 524288 | tf_op jit(solution)/shard_map/all_to_all | solution.py:321
  103.6 0.2 shard_map.91
  103.8 14.0 %all_to_all.80.u_ref = bf16[32,8,512]{2,1,0:T(8,128)(2,1)S(1)} all-to-all(bf16[32,8,512]{2,1,0:T(8,128)(2,1)S(1)} %shard_map.91), channel_id=1, replica_groups=mesh['x'=4,'y'=4,'z'=8,'c'=2] {'y','z'}, dimensions={0} | all-to-all | bytes 524288 | tf_op jit(solution)/shard_map/all_to_all | solution.py:321
  117.8 0.0 copy-done
  117.8 1.3 shard_map.92
  119.1 15.6 %all_to_all.81.pair_ref.took_ref = bf16[32,16,512]{2,1,0:T(8,128)(2,1)S(1)} all-to-all(bf16[32,16,512]{2,1,0:T(8,128)(2,1)S(1)} %get-tuple-element.75), channel_id=1, replica_groups=mesh['x'=4,'y'=4,'z'=8,'c'=2] {'y','z'}, dimensions={0} | all-to-all | bytes 1048576 | tf_op jit(solution)/shard_map/all_to_all | solution.py:321
  134.7 0.3 shard_map.93
  135.1 16.8 %all_to_all.82.pair_ref.gave_ref = bf16[32,16,512]{2,1,0:T(8,128)(2,1)S(1)} all-to-all(bf16[32,16,512]{2,1,0:T(8,128)(2,1)S(1)} %shard_map.93), channel_id=1, replica_groups=mesh['x'=4,'y'=4,'z'=8,'c'=2] {'y','z'}, dimensions={0} | all-to-all | bytes 1048576 | tf_op jit(solution)/shard_map/all_to_all | solution.py:321
  151.9 0.7 shard_map.94
  152.6 0.8 shard_map.95.held_ref
  153.4 14.9 %all_to_all.83.z_ref.gu_ref = bf16[32,8,512]{2,1,0:T(8,128)(2,1)S(1)} all-to-all(bf16[32,8,512]{2,1,0:T(8,128)(2,1)S(1)} %get-tuple-element.84), channel_id=1, replica_groups=mesh['x'=4,'y'=4,'z'=8,'c'=2] {'y','z'}, dimensions={0} | all-to-all | bytes 524288 | tf_op jit(solution)/shard_map/all_to_all | solution.py:321
  168.3 0.2 shard_map.96
  168.5 13.9 %all_to_all.84.gz_ref = bf16[32,8,512]{2,1,0:T(8,128)(2,1)S(1)} all-to-all(bf16[32,8,512]{2,1,0:T(8,128)(2,1)S(1)} %shard_map.96), channel_id=1, replica_groups=mesh['x'=4,'y'=4,'z'=8,'c'=2] {'y','z'}, dimensions={0} | all-to-all | bytes 524288 | tf_op jit(solution)/shard_map/all_to_all | solution.py:321
  182.5 0.5 shard_map.97
  183.0 0.8 shard_map.98.held_ref
  183.7 13.9 %all_to_all.85.z_ref.gu_ref = bf16[32,8,512]{2,1,0:T(8,128)(2,1)S(1)} all-to-all(bf16[32,8,512]{2,1,0:T(8,128)(2,1)S(1)} %get-tuple-element.92), channel_id=1, replica_groups=mesh['x'=4,'y'=4,'z'=8,'c'=2] {'y','z'}, dimensions={0} | all-to-all | bytes 524288 | tf_op jit(solution)/shard_map/all_to_all | solution.py:321
  197.6 0.2 shard_map.99
  197.9 15.1 %all_to_all.86.gz_ref = bf16[32,8,512]{2,1,0:T(8,128)(2,1)S(1)} all-to-all(bf16[32,8,512]{2,1,0:T(8,128)(2,1)S(1)} %shard_map.99), channel_id=1, replica_groups=mesh['x'=4,'y'=4,'z'=8,'c'=2] {'y','z'}, dimensions={0} | all-to-all | bytes 524288 | tf_op jit(solution)/shard_map/all_to_all | solution.py:321
  212.9 0.5 shard_map.100
  213.4 0.8 shard_map.101.held_ref
  214.2 15.6 %all_to_all.87.z_ref.gu_ref = bf16[32,8,512]{2,1,0:T(8,128)(2,1)S(1)} all-to-all(bf16[32,8,512]{2,1,0:T(8,128)(2,1)S(1)} %get-tuple-element.100), channel_id=1, replica_groups=mesh['x'=4,'y'=4,'z'=8,'c'=2] {'y','z'}, dimensions={0} | all-to-all | bytes 524288 | tf_op jit(solution)/shard_map/all_to_all | solution.py:321
  229.8 0.2 shard_map.102
  230.0 13.8 %all_to_all.88.gz_ref = bf16[32,8,512]{2,1,0:T(8,128)(2,1)S(1)} all-to-all(bf16[32,8,512]{2,1,0:T(8,128)(2,1)S(1)} %shard_map.102), channel_id=1, replica_groups=mesh['x'=4,'y'=4,'z'=8,'c'=2] {'y','z'}, dimensions={0} | all-to-all | bytes 524288 | tf_op jit(solution)/shard_map/all_to_all | solution.py:321
  243.8 0.9 shard_map.103
  244.8 16.0 %all_to_all.89.got_ref = bf16[4,2,832,128]{3,2,1,0:T(8,128)(2,1)S(1)} all-to-all(bf16[4,2,832,128]{3,2,1,0:T(8,128)(2,1)S(1)} %shard_map.103), channel_id=1, replica_groups=mesh['x'=4,'y'=4,'z'=8,'c'=2] {'x'}, dimensions={0} | all-to-all | bytes 3407872 | tf_op jit(solution)/shard_map/all_to_all | solution.py:407
  260.8 0.6 shard_map.104
  261.4 19.9 %collective-permute-start.6 = (bf16[4,832,128]{2,1,0:T(8,128)(2,1)S(1)}, bf16[4,832,128]{2,1,0:T(8,128)(2,1)S(1)}, u32[]{:S(2)}, u32[]{:S(2)}) collective-permute-start(bf16[4,832,128]{2,1,0:T(8,128)(2,1)S(1)} %shard_map.104), channel_id=1, source_target_pairs={{0,1},{1,0},{2,3},{3,2},{4,5},{5,4},{6,7},{7,6},{8,9},{9,8},{10,11... | collective-permute-start | bytes 2555912 | tf_op jit(solution)/shard_map/ppermute | solution.py:304
  281.3 2.0 collective-permute-done.6.other_ref
  283.3 1.7 shard_map.105
  (1 shorter events, 0.0 us)
Async XLA Ops:
  0.6 15.9 %copy-start.1 = (bf16[4096,128]{1,0:T(8,128)(2,1)S(1)}, bf16[4096,128]{1,0:T(8,128)(2,1)}, u32[]{:S(2)}) copy-start(bf16[4096,128]{1,0:T(8,128)(2,1)} %mine_ref.2) | copy-start | bytes 3145732
  2.3 5.3 %collective-permute-start.3 = (bf16[320,128]{1,0:T(8,128)(2,1)S(1)}, bf16[320,128]{1,0:T(8,128)(2,1)S(1)}, u32[]{:S(2)}, u32[]{:S(2)}) collective-permute-start(bf16[320,128]{1,0:T(8,128)(2,1)S(1)} %maximum_maximum_fusion.refs_0_), channel_id=1, source_target_pairs={{0,192},{64,0},{128,64},{192,128},{1,193},{65,1},{129,65},{193,129... | collective-permute-start | bytes 245768 | tf_op jit(solution)/shard_map/ppermute | solution.py:307
  5.6 4.9 %collective-permute-start.2 = (bf16[320,128]{1,0:T(8,128)(2,1)S(1)}, bf16[320,128]{1,0:T(8,128)(2,1)S(1)}, u32[]{:S(2)}, u32[]{:S(2)}) collective-permute-start(bf16[320,128]{1,0:T(8,128)(2,1)S(1)} %maximum_maximum_fusion.refs_0_), channel_id=1, source_target_pairs={{0,128},{64,192},{128,0},{192,64},{1,129},{65,193},{129,1},{193,65... | collective-permute-start | bytes 245768 | tf_op jit(solution)/shard_map/ppermute | solution.py:307
  6.2 6.4 %collective-permute-start.1 = (bf16[320,128]{1,0:T(8,128)(2,1)S(1)}, bf16[320,128]{1,0:T(8,128)(2,1)S(1)}, u32[]{:S(2)}, u32[]{:S(2)}) collective-permute-start(bf16[320,128]{1,0:T(8,128)(2,1)S(1)} %maximum_maximum_fusion.refs_0_), channel_id=1, source_target_pairs={{0,64},{64,128},{128,192},{192,0},{1,65},{65,129},{129,193},{193,1... | collective-permute-start | bytes 245768 | tf_op jit(solution)/shard_map/ppermute | solution.py:307
  12.6 4.7 %collective-permute-start.4 = (bf16[4,320,128]{2,1,0:T(8,128)(2,1)S(1)}, bf16[4,320,128]{2,1,0:T(8,128)(2,1)S(1)}, u32[]{:S(2)}, u32[]{:S(2)}) collective-permute-start(bf16[4,320,128]{2,1,0:T(8,128)(2,1)S(1)} %pad_maximum_fusion), channel_id=1, source_target_pairs={{0,1},{1,0},{2,3},{3,2},{4,5},{5,4},{6,7},{7,6},{8,9},{9,8},{10,11... | collective-permute-start | bytes 983048 | tf_op jit(solution)/shard_map/ppermute | solution.py:304
  14.8 1.7 collective-permute-start
  15.8 4.3 %collective-permute-start.5 = (bf16[512,128]{1,0:T(8,128)(2,1)S(1)}, bf16[512,128]{1,0:T(8,128)(2,1)S(1)}, u32[]{:S(2)}, u32[]{:S(2)}) collective-permute-start(bf16[512,128]{1,0:T(8,128)(2,1)S(1)} %constant_dynamic-slice_fusion), channel_id=1, source_target_pairs={{0,1},{1,0},{2,3},{3,2},{4,5},{5,4},{6,7},{7,6},{8,9},{9,8},{10,11... | collective-permute-start | bytes 393224 | tf_op jit(solution)/shard_map/ppermute | solution.py:304
  73.6 44.2 %copy-start = (bf16[4096,128]{1,0:T(8,128)(2,1)S(1)}, bf16[4096,128]{1,0:T(8,128)(2,1)}, u32[]{:S(2)}) copy-start(bf16[4096,128]{1,0:T(8,128)(2,1)} %mine_ref.3) | copy-start | bytes 3145732
  261.4 21.9 %collective-permute-start.6 = (bf16[4,832,128]{2,1,0:T(8,128)(2,1)S(1)}, bf16[4,832,128]{2,1,0:T(8,128)(2,1)S(1)}, u32[]{:S(2)}, u32[]{:S(2)}) collective-permute-start(bf16[4,832,128]{2,1,0:T(8,128)(2,1)S(1)} %shard_map.104), channel_id=1, source_target_pairs={{0,1},{1,0},{2,3},{3,2},{4,5},{5,4},{6,7},{7,6},{8,9},{9,8},{10,11... | collective-permute-start | bytes 2555912 | tf_op jit(solution)/shard_map/ppermute | solution.py:304

commit v5 on v4

--- a/solution.py
+++ b/solution.py
@@ -1,3 +1,5 @@
+import functools
+
 import jax
 import jax.numpy as jnp
 from jax import lax
@@ -84,14 +86,18 @@
         lt_out[...] = nt(left, q).astype(BF)
 
 
-def turned(core, mine_ref, other_ref):
+def turned(at_ref, whole_ref, other_ref):
+    core = at_ref[1]
+    n = other_ref.shape[0]
+    mine = whole_ref[pl.ds(pl.multiple_of(at_ref[2] * n, n), n), :]
+    other = other_ref[...]
     p = feature_order(256, 128, offset=core * 128)
     o = feature_order(256, 128, offset=128 - core * 128)
-    return (nt(p, mine_ref[...]) + nt(o, other_ref[...])).astype(BF)
+    return (nt(p, mine) + nt(o, other)).astype(BF)
 
 
 def turn_kernel(at_ref, mine_ref, other_ref, x_ref):
-    x_ref[...] = turned(at_ref[1], mine_ref, other_ref)
+    x_ref[...] = turned(at_ref, mine_ref, other_ref)
 
 
 def first_kernel(x_ref, rt_ref, z_ref):
@@ -124,7 +130,7 @@
     new = (x.astype(F32) + rows_of(u_ref) * sig).astype(BF)
     x_out[...] = new
     top = jax.nn.sigmoid(nn(gt_top_ref[...], new))
-    y = turned(at_ref[1], mine_ref, other_ref)
+    y = turned(at_ref, mine_ref, other_ref)
     y_out[...] = y
     put_rows(pair_ref, nn(rt_ref[...], new), y.astype(F32) * top)
 
@@ -183,35 +189,35 @@
     return parts
 
 
-def put_parts(parts, out_ref):
+def put_parts(parts, layer, out_ref):
     for c in range(2):
         start = 0
         for part in parts[c]:
             stop = start + part.shape[0]
-            out_ref[0, c, start:stop, :] = part.astype(BF)
+            out_ref[layer, c, start:stop, :] = part.astype(BF)
             start = stop
 
 
-def top_parts_kernel(x_ref, gave_ref, gg_ref, took_ref, y_ref, out_ref):
+def top_parts_kernel(layer, x_ref, gave_ref, gg_ref, took_ref, y_ref, out_ref):
     gz = rows_of(gave_ref, 1).astype(BF)
     z = rows_of(took_ref, 0).astype(BF)
     gu = rows_of(took_ref, 1).astype(BF)
-    put_parts(parts_of(x_ref[...], gz, gg_ref[...], z, gu, y_ref[...]), out_ref)
-
-
-def parts_kernel(x_ref, gz_ref, gg_ref, z_ref, gu_ref, y_ref, held_ref, out_ref):
+    put_parts(parts_of(x_ref[...], gz, gg_ref[...], z, gu, y_ref[...]), layer, out_ref)
+
+
+def parts_kernel(layer, x_ref, gz_ref, gg_ref, z_ref, gu_ref, y_ref, held_ref, out_ref):
     gz = rows_of(gz_ref).astype(BF)
     z = rows_of(z_ref).astype(BF)
     gu = rows_of(gu_ref).astype(BF)
-    put_parts(parts_of(x_ref[...], gz, gg_ref[...], z, gu, y_ref[...]), out_ref)
-
-
-def last_kernel(x_ref, gz_ref, gg_ref, z_ref, gu_ref, y_ref, r_ref, g_ref, held_ref, out_ref):
+    put_parts(parts_of(x_ref[...], gz, gg_ref[...], z, gu, y_ref[...]), layer, out_ref)
+
+
+def last_kernel(layer, x_ref, gz_ref, gg_ref, z_ref, gu_ref, y_ref, r_ref, g_ref, held_ref, out_ref):
     gz = rows_of(gz_ref).astype(BF)
     z = rows_of(z_ref).astype(BF)
     gu = rows_of(gu_ref).astype(BF)
     lower = lower_of(y_ref[...], gz, gg_ref[...], r_ref[...], g_ref[...])
-    put_parts(parts_of(x_ref[...], gz, gg_ref[...], z, gu, lower), out_ref)
+    put_parts(parts_of(x_ref[...], gz, gg_ref[...], z, gu, lower), layer, out_ref)
 
 
 def pick_kernel(at_ref, got_ref, out_ref):
@@ -236,57 +242,28 @@
     l_out[1] = total[256:, 64:]
 
 
-def run(kernel, outs, *args, dots=1, at=None, scratch=(), blocks=None):
+def run(kernel, outs, *args, dots=1, at=None, scratch=(), aliases=None):
     nbytes = sum(a.size * a.dtype.itemsize for a in args)
-    params = pltpu.CompilerParams(vmem_limit_bytes=16 << 20)
-    cost = pl.CostEstimate(
-        flops=dots * 2 * 256 * 256 * 512, bytes_accessed=2 * nbytes, transcendentals=0
-    )
-    if at is None:
-        return pl.pallas_call(
-            kernel, out_shape=outs, compiler_params=params, cost_estimate=cost
-        )(*args)
-    specs = [
-        spec or pl.BlockSpec(a.shape, lambda i, at, nd=a.ndim: (0,) * nd)
-        for a, spec in zip(args, blocks or [None] * len(args))
-    ]
-    many = isinstance(outs, list)
-    out_specs = [
-        pl.BlockSpec(o.shape, lambda i, at, nd=len(o.shape): (0,) * nd)
-        for o in (outs if many else [outs])
-    ]
+    specs = [pl.BlockSpec(memory_space=pltpu.VMEM)] * len(args)
+    if at is not None:
+        args = (at,) + args
+        specs = [pl.BlockSpec(memory_space=pltpu.SMEM)] + specs
     return pl.pallas_call(
         kernel,
         out_shape=outs,
-        grid_spec=pltpu.PrefetchScalarGridSpec(
-            num_scalar_prefetch=1,
-            grid=(1,),
-            in_specs=specs,
-            out_specs=out_specs if many else out_specs[0],
-            scratch_shapes=list(scratch),
-        ),
-        compiler_params=params,
-        cost_estimate=cost,
-    )(at, *args)
-
-
-def run_parts(kernel, layer, whole, *args):
-    more = {} if layer == 3 else {"input_output_aliases": {len(args) - 1: 0}}
-    specs = [pl.BlockSpec(a.shape, lambda i, nd=a.ndim: (0,) * nd) for a in args]
-    if layer != 3:
-        specs[-1] = pl.BlockSpec(memory_space=pl.ANY)
-    return pl.pallas_call(
-        kernel,
-        out_shape=whole,
-        grid=(1,),
         in_specs=specs,
-        out_specs=pl.BlockSpec((1,) + whole.shape[1:], lambda i: (layer, 0, 0, 0)),
+        scratch_shapes=list(scratch),
+        input_output_aliases=aliases or {},
         compiler_params=pltpu.CompilerParams(vmem_limit_bytes=16 << 20),
         cost_estimate=pl.CostEstimate(
-            flops=18 * 256 * 256 * 512, bytes_accessed=3 << 20, transcendentals=0
+            flops=dots * 2 * 256 * 256 * 512, bytes_accessed=2 * nbytes, transcendentals=0
         ),
-        **more,
     )(*args)
+
+
+def run_parts(kernel, layer, whole, *args):
+    aliases = {} if layer == 3 else {len(args) - 1: 0}
+    return run(functools.partial(kernel, layer), whole, *args, dots=9, aliases=aliases)
 
 
 def sds(*shape, dtype=BF):
@@ -322,7 +299,6 @@
 
     flat = sds(256, tokens)
     sent = sds(32, 8, tokens)
-    mine = pl.BlockSpec((tokens, 128), lambda i, at: (at[2], 0))
     outs = run(
         prepare_kernel,
         [sds(256, 256)] * 24,
@@ -334,7 +310,7 @@
     )
     mats = [outs[6 * s : 6 * s + 6] for s in range(sections)]
     from_other = sent_over(inputs)
-    x0 = run(turn_kernel, flat, inputs, from_other, at=at, blocks=[mine, None])
+    x0 = run(turn_kernel, flat, inputs, from_other, at=at)
     z = run(first_kernel, sent, x0, mats[0][1])
     crossed = sent_over(cotangent)
     z, crossed = lax.optimization_barrier((z, crossed))
@@ -362,7 +338,6 @@
                 mats[last][3],
                 dots=4,
                 at=at,
-                blocks=[None, None, None, None, mine, None, None],
             )
         x.append(new)
     took = swap(both)

time: 286 us -> 286 us (level)
  no operation moved by 1% of the time
where the time goes in v5:
time: 286 us; the launch traced here: 285 us
  blocking collectives  232 us (81%)
  starting transfers between devices  26.3 us (9%)
  Pallas kernels  14.6 us (5%)
  waiting for transfers between devices  6.96 us (2%)
    all_to_all x14, blocking collectives, swap(): return lax.all_to_all(block, ('y', 'z'), 0, 0, tiled=True)  216 us
    ppermute x4, starting transfers between devices, to_other(): return lax.ppermute(value, 'c', [(0, 1), (1, 0)])  21.9 us
    all_to_all x1, blocking collectives, program(): got = lax.all_to_all(parts, 'x', 0, 0, tiled=True)  16 us
    pallas_call x22, Pallas kernels, run(): pl.pallas_call(kernel, out_shape=outs, in_specs=specs, scratch_shapes=lis...  14.6 us
  transfers between devices with their start and end apart: 7, of which 3 were waited for; matrix products, arithmetic and copies ran while one was open for 1% of the time, Pallas kernels for 1%

profile of v5, /device:TPU:1, one launch (start us, length us, event | category | flops | bytes accessed | tf_op | source)
XLA Modules:
  0.0 284.9 jit_solution(16113434296515917311)
XLA Ops:
  0.6 0.0 copy-start.1
  0.6 0.8 slice_bitcast_fusion.1
  1.5 0.9 maximum_maximum_fusion.refs_0_
  2.3 3.3 %collective-permute-start.3 = (bf16[320,128]{1,0:T(8,128)(2,1)S(1)}, bf16[320,128]{1,0:T(8,128)(2,1)S(1)}, u32[]{:S(2)}, u32[]{:S(2)}) collective-permute-start(bf16[320,128]{1,0:T(8,128)(2,1)S(1)} %maximum_maximum_fusion.refs_0_), channel_id=1, source_target_pairs={{0,192},{64,0},{128,64},{192,128},{1,193},{65,1},{129,65},{193,129... | collective-permute-start | bytes 245768 | tf_op jit(solution)/shard_map/ppermute | solution.py:284
  5.6 0.5 collective-permute-start.2
  6.2 0.6 collective-permute-start.1
  6.8 0.9 fusion
  7.6 0.0 collective-permute-done.3.refs_3_
  7.6 2.9 %collective-permute-done.2.refs_2_ = bf16[320,128]{1,0:T(8,128)(2,1)S(1)} collective-permute-done((bf16[320,128]{1,0:T(8,128)(2,1)S(1)}, bf16[320,128]{1,0:T(8,128)(2,1)S(1)}, u32[]{:S(2)}, u32[]{:S(2)}) %collective-permute-start.2) | collective-permute-done | bytes 81952 | tf_op jit(solution)/shard_map/ppermute | solution.py:284
  10.5 2.1 collective-permute-done.1.refs_1_
  12.6 1.3 collective-permute-start.4
  13.9 0.9 constant_dynamic-slice_fusion.1
  14.8 0.1 collective-permute-start
  14.9 0.9 constant_dynamic-slice_fusion
  15.8 0.6 collective-permute-start.5
  16.4 0.1 pad_add_fusion.at_ref
  16.5 0.0 collective-permute-done.other_ref
  16.5 0.0 copy-done.1
  16.5 0.8 shard_map.84.x_ref
  17.4 0.0 collective-permute-done.4.refs_4_
  17.4 2.5 shard_map.85
  19.9 0.2 shard_map.86
  20.1 0.0 collective-permute-done.5.other_ref
  20.1 21.3 %all_to_all.75.z_ref = bf16[32,8,512]{2,1,0:T(8,128)(2,1)S(1)} all-to-all(bf16[32,8,512]{2,1,0:T(8,128)(2,1)S(1)} %shard_map.86), channel_id=1, replica_groups=mesh['x'=4,'y'=4,'z'=8,'c'=2] {'y','z'}, dimensions={0} | all-to-all | bytes 524288 | tf_op jit(solution)/shard_map/all_to_all | solution.py:298
  41.4 0.2 shard_map.87
  41.6 15.9 %all_to_all.76.u_ref = bf16[32,8,512]{2,1,0:T(8,128)(2,1)S(1)} all-to-all(bf16[32,8,512]{2,1,0:T(8,128)(2,1)S(1)} %shard_map.87), channel_id=1, replica_groups=mesh['x'=4,'y'=4,'z'=8,'c'=2] {'y','z'}, dimensions={0} | all-to-all | bytes 524288 | tf_op jit(solution)/shard_map/all_to_all | solution.py:298
  57.5 0.5 shard_map.88
  58.0 15.6 %all_to_all.77.z_ref = bf16[32,8,512]{2,1,0:T(8,128)(2,1)S(1)} all-to-all(bf16[32,8,512]{2,1,0:T(8,128)(2,1)S(1)} %get-tuple-element.63), channel_id=1, replica_groups=mesh['x'=4,'y'=4,'z'=8,'c'=2] {'y','z'}, dimensions={0} | all-to-all | bytes 524288 | tf_op jit(solution)/shard_map/all_to_all | solution.py:298
  73.6 0.0 copy-start
  73.6 0.2 shard_map.89
  73.8 14.9 %all_to_all.78.u_ref = bf16[32,8,512]{2,1,0:T(8,128)(2,1)S(1)} all-to-all(bf16[32,8,512]{2,1,0:T(8,128)(2,1)S(1)} %shard_map.89), channel_id=1, replica_groups=mesh['x'=4,'y'=4,'z'=8,'c'=2] {'y','z'}, dimensions={0} | all-to-all | bytes 524288 | tf_op jit(solution)/shard_map/all_to_all | solution.py:298
  88.8 0.5 shard_map.90
  89.2 14.1 %all_to_all.79.z_ref = bf16[32,8,512]{2,1,0:T(8,128)(2,1)S(1)} all-to-all(bf16[32,8,512]{2,1,0:T(8,128)(2,1)S(1)} %get-tuple-element.68), channel_id=1, replica_groups=mesh['x'=4,'y'=4,'z'=8,'c'=2] {'y','z'}, dimensions={0} | all-to-all | bytes 524288 | tf_op jit(solution)/shard_map/all_to_all | solution.py:298
  103.4 0.2 shard_map.91
  103.6 14.2 %all_to_all.80.u_ref = bf16[32,8,512]{2,1,0:T(8,128)(2,1)S(1)} all-to-all(bf16[32,8,512]{2,1,0:T(8,128)(2,1)S(1)} %shard_map.91), channel_id=1, replica_groups=mesh['x'=4,'y'=4,'z'=8,'c'=2] {'y','z'}, dimensions={0} | all-to-all | bytes 524288 | tf_op jit(solution)/shard_map/all_to_all | solution.py:298
  117.8 0.0 copy-done
  117.8 1.2 shard_map.92
  119.0 15.6 %all_to_all.81.pair_ref.took_ref = bf16[32,16,512]{2,1,0:T(8,128)(2,1)S(1)} all-to-all(bf16[32,16,512]{2,1,0:T(8,128)(2,1)S(1)} %get-tuple-element.75), channel_id=1, replica_groups=mesh['x'=4,'y'=4,'z'=8,'c'=2] {'y','z'}, dimensions={0} | all-to-all | bytes 1048576 | tf_op jit(solution)/shard_map/all_to_all | solution.py:298
  134.6 0.3 shard_map.93
  134.9 16.9 %all_to_all.82.pair_ref.gave_ref = bf16[32,16,512]{2,1,0:T(8,128)(2,1)S(1)} all-to-all(bf16[32,16,512]{2,1,0:T(8,128)(2,1)S(1)} %shard_map.93), channel_id=1, replica_groups=mesh['x'=4,'y'=4,'z'=8,'c'=2] {'y','z'}, dimensions={0} | all-to-all | bytes 1048576 | tf_op jit(solution)/shard_map/all_to_all | solution.py:298
  151.8 0.7 shard_map.94
  152.5 0.8 shard_map.95.held_ref
  153.3 15.1 %all_to_all.83.z_ref.gu_ref = bf16[32,8,512]{2,1,0:T(8,128)(2,1)S(1)} all-to-all(bf16[32,8,512]{2,1,0:T(8,128)(2,1)S(1)} %get-tuple-element.84), channel_id=1, replica_groups=mesh['x'=4,'y'=4,'z'=8,'c'=2] {'y','z'}, dimensions={0} | all-to-all | bytes 524288 | tf_op jit(solution)/shard_map/all_to_all | solution.py:298
  168.3 0.2 shard_map.96
  168.5 13.9 %all_to_all.84.gz_ref = bf16[32,8,512]{2,1,0:T(8,128)(2,1)S(1)} all-to-all(bf16[32,8,512]{2,1,0:T(8,128)(2,1)S(1)} %shard_map.96), channel_id=1, replica_groups=mesh['x'=4,'y'=4,'z'=8,'c'=2] {'y','z'}, dimensions={0} | all-to-all | bytes 524288 | tf_op jit(solution)/shard_map/all_to_all | solution.py:298
  182.5 0.5 shard_map.97
  183.0 0.8 shard_map.98.held_ref
  183.7 13.9 %all_to_all.85.z_ref.gu_ref = bf16[32,8,512]{2,1,0:T(8,128)(2,1)S(1)} all-to-all(bf16[32,8,512]{2,1,0:T(8,128)(2,1)S(1)} %get-tuple-element.92), channel_id=1, replica_groups=mesh['x'=4,'y'=4,'z'=8,'c'=2] {'y','z'}, dimensions={0} | all-to-all | bytes 524288 | tf_op jit(solution)/shard_map/all_to_all | solution.py:298
  197.6 0.2 shard_map.99
  197.9 15.0 %all_to_all.86.gz_ref = bf16[32,8,512]{2,1,0:T(8,128)(2,1)S(1)} all-to-all(bf16[32,8,512]{2,1,0:T(8,128)(2,1)S(1)} %shard_map.99), channel_id=1, replica_groups=mesh['x'=4,'y'=4,'z'=8,'c'=2] {'y','z'}, dimensions={0} | all-to-all | bytes 524288 | tf_op jit(solution)/shard_map/all_to_all | solution.py:298
  212.9 0.5 shard_map.100
  213.4 0.8 shard_map.101.held_ref
  214.2 15.6 %all_to_all.87.z_ref.gu_ref = bf16[32,8,512]{2,1,0:T(8,128)(2,1)S(1)} all-to-all(bf16[32,8,512]{2,1,0:T(8,128)(2,1)S(1)} %get-tuple-element.100), channel_id=1, replica_groups=mesh['x'=4,'y'=4,'z'=8,'c'=2] {'y','z'}, dimensions={0} | all-to-all | bytes 524288 | tf_op jit(solution)/shard_map/all_to_all | solution.py:298
  229.8 0.2 shard_map.102
  230.0 13.8 %all_to_all.88.gz_ref = bf16[32,8,512]{2,1,0:T(8,128)(2,1)S(1)} all-to-all(bf16[32,8,512]{2,1,0:T(8,128)(2,1)S(1)} %shard_map.102), channel_id=1, replica_groups=mesh['x'=4,'y'=4,'z'=8,'c'=2] {'y','z'}, dimensions={0} | all-to-all | bytes 524288 | tf_op jit(solution)/shard_map/all_to_all | solution.py:298
  243.8 0.9 shard_map.103
  244.7 16.0 %all_to_all.89.got_ref = bf16[4,2,832,128]{3,2,1,0:T(8,128)(2,1)S(1)} all-to-all(bf16[4,2,832,128]{3,2,1,0:T(8,128)(2,1)S(1)} %shard_map.103), channel_id=1, replica_groups=mesh['x'=4,'y'=4,'z'=8,'c'=2] {'x'}, dimensions={0} | all-to-all | bytes 3407872 | tf_op jit(solution)/shard_map/all_to_all | solution.py:382
  260.7 0.6 shard_map.104
  261.3 19.9 %collective-permute-start.6 = (bf16[4,832,128]{2,1,0:T(8,128)(2,1)S(1)}, bf16[4,832,128]{2,1,0:T(8,128)(2,1)S(1)}, u32[]{:S(2)}, u32[]{:S(2)}) collective-permute-start(bf16[4,832,128]{2,1,0:T(8,128)(2,1)S(1)} %shard_map.104), channel_id=1, source_target_pairs={{0,1},{1,0},{2,3},{3,2},{4,5},{5,4},{6,7},{7,6},{8,9},{9,8},{10,11... | collective-permute-start | bytes 2555912 | tf_op jit(solution)/shard_map/ppermute | solution.py:281
  281.3 2.0 collective-permute-done.6.other_ref
  283.3 1.7 shard_map.105
  (1 shorter events, 0.0 us)
Async XLA Ops:
  0.6 15.9 %copy-start.1 = (bf16[4096,128]{1,0:T(8,128)(2,1)S(1)}, bf16[4096,128]{1,0:T(8,128)(2,1)}, u32[]{:S(2)}) copy-start(bf16[4096,128]{1,0:T(8,128)(2,1)} %mine_ref.2) | copy-start | bytes 3145732
  2.3 5.3 %collective-permute-start.3 = (bf16[320,128]{1,0:T(8,128)(2,1)S(1)}, bf16[320,128]{1,0:T(8,128)(2,1)S(1)}, u32[]{:S(2)}, u32[]{:S(2)}) collective-permute-start(bf16[320,128]{1,0:T(8,128)(2,1)S(1)} %maximum_maximum_fusion.refs_0_), channel_id=1, source_target_pairs={{0,192},{64,0},{128,64},{192,128},{1,193},{65,1},{129,65},{193,129... | collective-permute-start | bytes 245768 | tf_op jit(solution)/shard_map/ppermute | solution.py:284
  5.6 4.9 %collective-permute-start.2 = (bf16[320,128]{1,0:T(8,128)(2,1)S(1)}, bf16[320,128]{1,0:T(8,128)(2,1)S(1)}, u32[]{:S(2)}, u32[]{:S(2)}) collective-permute-start(bf16[320,128]{1,0:T(8,128)(2,1)S(1)} %maximum_maximum_fusion.refs_0_), channel_id=1, source_target_pairs={{0,128},{64,192},{128,0},{192,64},{1,129},{65,193},{129,1},{193,65... | collective-permute-start | bytes 245768 | tf_op jit(solution)/shard_map/ppermute | solution.py:284
  6.2 6.4 %collective-permute-start.1 = (bf16[320,128]{1,0:T(8,128)(2,1)S(1)}, bf16[320,128]{1,0:T(8,128)(2,1)S(1)}, u32[]{:S(2)}, u32[]{:S(2)}) collective-permute-start(bf16[320,128]{1,0:T(8,128)(2,1)S(1)} %maximum_maximum_fusion.refs_0_), channel_id=1, source_target_pairs={{0,64},{64,128},{128,192},{192,0},{1,65},{65,129},{129,193},{193,1... | collective-permute-start | bytes 245768 | tf_op jit(solution)/shard_map/ppermute | solution.py:284
  12.6 4.7 %collective-permute-start.4 = (bf16[4,320,128]{2,1,0:T(8,128)(2,1)S(1)}, bf16[4,320,128]{2,1,0:T(8,128)(2,1)S(1)}, u32[]{:S(2)}, u32[]{:S(2)}) collective-permute-start(bf16[4,320,128]{2,1,0:T(8,128)(2,1)S(1)} %pad_maximum_fusion), channel_id=1, source_target_pairs={{0,1},{1,0},{2,3},{3,2},{4,5},{5,4},{6,7},{7,6},{8,9},{9,8},{10,11... | collective-permute-start | bytes 983048 | tf_op jit(solution)/shard_map/ppermute | solution.py:281
  14.8 1.7 collective-permute-start
  15.8 4.3 %collective-permute-start.5 = (bf16[512,128]{1,0:T(8,128)(2,1)S(1)}, bf16[512,128]{1,0:T(8,128)(2,1)S(1)}, u32[]{:S(2)}, u32[]{:S(2)}) collective-permute-start(bf16[512,128]{1,0:T(8,128)(2,1)S(1)} %constant_dynamic-slice_fusion), channel_id=1, source_target_pairs={{0,1},{1,0},{2,3},{3,2},{4,5},{5,4},{6,7},{7,6},{8,9},{9,8},{10,11... | collective-permute-start | bytes 393224 | tf_op jit(solution)/shard_map/ppermute | solution.py:281
  73.6 44.2 %copy-start = (bf16[4096,128]{1,0:T(8,128)(2,1)S(1)}, bf16[4096,128]{1,0:T(8,128)(2,1)}, u32[]{:S(2)}) copy-start(bf16[4096,128]{1,0:T(8,128)(2,1)} %mine_ref.3) | copy-start | bytes 3145732
  261.3 21.9 %collective-permute-start.6 = (bf16[4,832,128]{2,1,0:T(8,128)(2,1)S(1)}, bf16[4,832,128]{2,1,0:T(8,128)(2,1)S(1)}, u32[]{:S(2)}, u32[]{:S(2)}) collective-permute-start(bf16[4,832,128]{2,1,0:T(8,128)(2,1)S(1)} %shard_map.104), channel_id=1, source_target_pairs={{0,1},{1,0},{2,3},{3,2},{4,5},{5,4},{6,7},{7,6},{8,9},{9,8},{10,11... | collective-permute-start | bytes 2555912 | tf_op jit(solution)/shard_map/ppermute | solution.py:281

commit v6 on v5

--- a/solution.py
+++ b/solution.py
@@ -19,17 +19,21 @@
     return lax.dot_general(a, b, (((1,), (1,)), ((), ())), preferred_element_type=F32)
 
 
+def place_of(slot):
+    return (slot & 3) * 8 + (slot >> 2)
+
+
 def feature_order(rows, cols, transposed=False, offset=0):
     r = lax.broadcasted_iota(jnp.int32, (rows, cols), 1 if transposed else 0)
     c = lax.broadcasted_iota(jnp.int32, (rows, cols), 0 if transposed else 1)
-    natural = ((r >> 2) & 1) * 128 + (r >> 3) * 4 + (r & 3)
+    natural = ((r >> 2) & 1) * 128 + place_of(r >> 3) * 4 + (r & 3)
     return jnp.where(natural == c + offset, 1.0, 0.0).astype(BF)
 
 
 def position_order(rows, cols, transposed=False):
     r = lax.broadcasted_iota(jnp.int32, (rows, cols), 1 if transposed else 0)
     c = lax.broadcasted_iota(jnp.int32, (rows, cols), 0 if transposed else 1)
-    natural = (r & 3) * 64 + (r >> 3) * 2 + ((r >> 2) & 1)
+    natural = (r & 3) * 64 + place_of(r >> 3) * 2 + ((r >> 2) & 1)
     return jnp.where(natural == c, 1.0, 0.0).astype(BF)
 
 
@@ -295,7 +299,7 @@
         return to_other(lax.dynamic_slice_in_dim(whole, start, tokens, 0))
 
     def swap(block):
-        return lax.all_to_all(block, ("y", "z"), 0, 0, tiled=True)
+        return lax.all_to_all(block, ("z", "y"), 0, 0, tiled=True)
 
     flat = sds(256, tokens)
     sent = sds(32, 8, tokens)

time: 286 us -> 285 us (level)
  no operation moved by 1% of the time
where the time goes in v6:
time: 285 us; the launch traced here: 284 us
  blocking collectives  232 us (81%)
  starting transfers between devices  25.6 us (9%)
  Pallas kernels  14.6 us (5%)
  waiting for transfers between devices  6.96 us (2%)
    all_to_all x14, blocking collectives, swap(): return lax.all_to_all(block, ('z', 'y'), 0, 0, tiled=True)  216 us
    ppermute x4, starting transfers between devices, to_other(): return lax.ppermute(value, 'c', [(0, 1), (1, 0)])  21.1 us
    all_to_all x1, blocking collectives, program(): got = lax.all_to_all(parts, 'x', 0, 0, tiled=True)  16 us
    pallas_call x22, Pallas kernels, run(): pl.pallas_call(kernel, out_shape=outs, in_specs=specs, scratch_shapes=lis...  14.6 us
  transfers between devices with their start and end apart: 7, of which 3 were waited for; matrix products, arithmetic and copies ran while one was open for 1% of the time, Pallas kernels for 1%

profile of v6, /device:TPU:1, one launch (start us, length us, event | category | flops | bytes accessed | tf_op | source)
XLA Modules:
  0.0 284.4 jit_solution(3253909810957310172)
XLA Ops:
  0.6 0.0 copy-start.1
  0.6 0.8 slice_bitcast_fusion.1
  1.5 0.9 maximum_maximum_fusion.refs_0_
  2.3 3.3 %collective-permute-start.3 = (bf16[320,128]{1,0:T(8,128)(2,1)S(1)}, bf16[320,128]{1,0:T(8,128)(2,1)S(1)}, u32[]{:S(2)}, u32[]{:S(2)}) collective-permute-start(bf16[320,128]{1,0:T(8,128)(2,1)S(1)} %maximum_maximum_fusion.refs_0_), channel_id=1, source_target_pairs={{0,192},{64,0},{128,64},{192,128},{1,193},{65,1},{129,65},{193,129... | collective-permute-start | bytes 245768 | tf_op jit(solution)/shard_map/ppermute | solution.py:288
  5.6 0.5 collective-permute-start.2
  6.2 0.6 collective-permute-start.1
  6.8 0.9 fusion
  7.6 0.0 collective-permute-done.3.refs_3_
  7.6 2.9 %collective-permute-done.2.refs_2_ = bf16[320,128]{1,0:T(8,128)(2,1)S(1)} collective-permute-done((bf16[320,128]{1,0:T(8,128)(2,1)S(1)}, bf16[320,128]{1,0:T(8,128)(2,1)S(1)}, u32[]{:S(2)}, u32[]{:S(2)}) %collective-permute-start.2) | collective-permute-done | bytes 81952 | tf_op jit(solution)/shard_map/ppermute | solution.py:288
  10.5 2.1 collective-permute-done.1.refs_1_
  12.6 1.3 collective-permute-start.4
  13.9 0.9 constant_dynamic-slice_fusion.1
  14.8 0.1 collective-permute-start
  14.9 0.9 constant_dynamic-slice_fusion
  15.8 0.6 collective-permute-start.5
  16.4 0.1 pad_add_fusion.at_ref
  16.5 0.0 collective-permute-done.other_ref
  16.5 0.0 copy-done.1
  16.5 0.8 shard_map.84.x_ref
  17.4 0.0 collective-permute-done.4.refs_4_
  17.4 2.5 shard_map.85
  19.9 0.2 shard_map.86
  20.1 0.0 collective-permute-done.5.other_ref
  20.1 22.9 %all_to_all.75.z_ref = bf16[32,8,512]{2,1,0:T(8,128)(2,1)S(1)} all-to-all(bf16[32,8,512]{2,1,0:T(8,128)(2,1)S(1)} %shard_map.86), channel_id=1, replica_groups=mesh['x'=4,'y'=4,'z'=8,'c'=2] {'z','y'}, dimensions={0} | all-to-all | bytes 524288 | tf_op jit(solution)/shard_map/all_to_all | solution.py:302
  43.1 0.2 shard_map.87
  43.3 14.7 %all_to_all.76.u_ref = bf16[32,8,512]{2,1,0:T(8,128)(2,1)S(1)} all-to-all(bf16[32,8,512]{2,1,0:T(8,128)(2,1)S(1)} %shard_map.87), channel_id=1, replica_groups=mesh['x'=4,'y'=4,'z'=8,'c'=2] {'z','y'}, dimensions={0} | all-to-all | bytes 524288 | tf_op jit(solution)/shard_map/all_to_all | solution.py:302
  58.0 0.5 shard_map.88
  58.5 15.3 %all_to_all.77.z_ref = bf16[32,8,512]{2,1,0:T(8,128)(2,1)S(1)} all-to-all(bf16[32,8,512]{2,1,0:T(8,128)(2,1)S(1)} %get-tuple-element.63), channel_id=1, replica_groups=mesh['x'=4,'y'=4,'z'=8,'c'=2] {'z','y'}, dimensions={0} | all-to-all | bytes 524288 | tf_op jit(solution)/shard_map/all_to_all | solution.py:302
  73.8 0.0 copy-start
  73.8 0.2 shard_map.89
  74.0 14.7 %all_to_all.78.u_ref = bf16[32,8,512]{2,1,0:T(8,128)(2,1)S(1)} all-to-all(bf16[32,8,512]{2,1,0:T(8,128)(2,1)S(1)} %shard_map.89), channel_id=1, replica_groups=mesh['x'=4,'y'=4,'z'=8,'c'=2] {'z','y'}, dimensions={0} | all-to-all | bytes 524288 | tf_op jit(solution)/shard_map/all_to_all | solution.py:302
  88.7 0.5 shard_map.90
  89.2 14.1 %all_to_all.79.z_ref = bf16[32,8,512]{2,1,0:T(8,128)(2,1)S(1)} all-to-all(bf16[32,8,512]{2,1,0:T(8,128)(2,1)S(1)} %get-tuple-element.68), channel_id=1, replica_groups=mesh['x'=4,'y'=4,'z'=8,'c'=2] {'z','y'}, dimensions={0} | all-to-all | bytes 524288 | tf_op jit(solution)/shard_map/all_to_all | solution.py:302
  103.2 0.2 shard_map.91
  103.5 13.8 %all_to_all.80.u_ref = bf16[32,8,512]{2,1,0:T(8,128)(2,1)S(1)} all-to-all(bf16[32,8,512]{2,1,0:T(8,128)(2,1)S(1)} %shard_map.91), channel_id=1, replica_groups=mesh['x'=4,'y'=4,'z'=8,'c'=2] {'z','y'}, dimensions={0} | all-to-all | bytes 524288 | tf_op jit(solution)/shard_map/all_to_all | solution.py:302
  117.3 0.0 copy-done
  117.3 1.3 shard_map.92
  118.6 16.1 %all_to_all.81.pair_ref.took_ref = bf16[32,16,512]{2,1,0:T(8,128)(2,1)S(1)} all-to-all(bf16[32,16,512]{2,1,0:T(8,128)(2,1)S(1)} %get-tuple-element.75), channel_id=1, replica_groups=mesh['x'=4,'y'=4,'z'=8,'c'=2] {'z','y'}, dimensions={0} | all-to-all | bytes 1048576 | tf_op jit(solution)/shard_map/all_to_all | solution.py:302
  134.7 0.3 shard_map.93
  135.0 16.7 %all_to_all.82.pair_ref.gave_ref = bf16[32,16,512]{2,1,0:T(8,128)(2,1)S(1)} all-to-all(bf16[32,16,512]{2,1,0:T(8,128)(2,1)S(1)} %shard_map.93), channel_id=1, replica_groups=mesh['x'=4,'y'=4,'z'=8,'c'=2] {'z','y'}, dimensions={0} | all-to-all | bytes 1048576 | tf_op jit(solution)/shard_map/all_to_all | solution.py:302
  151.7 0.7 shard_map.94
  152.4 0.8 shard_map.95.held_ref
  153.2 14.1 %all_to_all.83.z_ref.gu_ref = bf16[32,8,512]{2,1,0:T(8,128)(2,1)S(1)} all-to-all(bf16[32,8,512]{2,1,0:T(8,128)(2,1)S(1)} %get-tuple-element.84), channel_id=1, replica_groups=mesh['x'=4,'y'=4,'z'=8,'c'=2] {'z','y'}, dimensions={0} | all-to-all | bytes 524288 | tf_op jit(solution)/shard_map/all_to_all | solution.py:302
  167.3 0.2 shard_map.96
  167.6 14.0 %all_to_all.84.gz_ref = bf16[32,8,512]{2,1,0:T(8,128)(2,1)S(1)} all-to-all(bf16[32,8,512]{2,1,0:T(8,128)(2,1)S(1)} %shard_map.96), channel_id=1, replica_groups=mesh['x'=4,'y'=4,'z'=8,'c'=2] {'z','y'}, dimensions={0} | all-to-all | bytes 524288 | tf_op jit(solution)/shard_map/all_to_all | solution.py:302
  181.6 0.5 shard_map.97
  182.1 0.8 shard_map.98.held_ref
  182.9 13.7 %all_to_all.85.z_ref.gu_ref = bf16[32,8,512]{2,1,0:T(8,128)(2,1)S(1)} all-to-all(bf16[32,8,512]{2,1,0:T(8,128)(2,1)S(1)} %get-tuple-element.92), channel_id=1, replica_groups=mesh['x'=4,'y'=4,'z'=8,'c'=2] {'z','y'}, dimensions={0} | all-to-all | bytes 524288 | tf_op jit(solution)/shard_map/all_to_all | solution.py:302
  196.6 0.2 shard_map.99
  196.8 15.4 %all_to_all.86.gz_ref = bf16[32,8,512]{2,1,0:T(8,128)(2,1)S(1)} all-to-all(bf16[32,8,512]{2,1,0:T(8,128)(2,1)S(1)} %shard_map.99), channel_id=1, replica_groups=mesh['x'=4,'y'=4,'z'=8,'c'=2] {'z','y'}, dimensions={0} | all-to-all | bytes 524288 | tf_op jit(solution)/shard_map/all_to_all | solution.py:302
  212.1 0.5 shard_map.100
  212.6 0.8 shard_map.101.held_ref
  213.4 16.0 %all_to_all.87.z_ref.gu_ref = bf16[32,8,512]{2,1,0:T(8,128)(2,1)S(1)} all-to-all(bf16[32,8,512]{2,1,0:T(8,128)(2,1)S(1)} %get-tuple-element.100), channel_id=1, replica_groups=mesh['x'=4,'y'=4,'z'=8,'c'=2] {'z','y'}, dimensions={0} | all-to-all | bytes 524288 | tf_op jit(solution)/shard_map/all_to_all | solution.py:302
  229.4 0.2 shard_map.102
  229.7 14.4 %all_to_all.88.gz_ref = bf16[32,8,512]{2,1,0:T(8,128)(2,1)S(1)} all-to-all(bf16[32,8,512]{2,1,0:T(8,128)(2,1)S(1)} %shard_map.102), channel_id=1, replica_groups=mesh['x'=4,'y'=4,'z'=8,'c'=2] {'z','y'}, dimensions={0} | all-to-all | bytes 524288 | tf_op jit(solution)/shard_map/all_to_all | solution.py:302
  244.1 0.9 shard_map.103
  245.0 16.0 %all_to_all.89.got_ref = bf16[4,2,832,128]{3,2,1,0:T(8,128)(2,1)S(1)} all-to-all(bf16[4,2,832,128]{3,2,1,0:T(8,128)(2,1)S(1)} %shard_map.103), channel_id=1, replica_groups=mesh['x'=4,'y'=4,'z'=8,'c'=2] {'x'}, dimensions={0} | all-to-all | bytes 3407872 | tf_op jit(solution)/shard_map/all_to_all | solution.py:386
  261.0 0.6 shard_map.104
  261.6 19.2 %collective-permute-start.6 = (bf16[4,832,128]{2,1,0:T(8,128)(2,1)S(1)}, bf16[4,832,128]{2,1,0:T(8,128)(2,1)S(1)}, u32[]{:S(2)}, u32[]{:S(2)}) collective-permute-start(bf16[4,832,128]{2,1,0:T(8,128)(2,1)S(1)} %shard_map.104), channel_id=1, source_target_pairs={{0,1},{1,0},{2,3},{3,2},{4,5},{5,4},{6,7},{7,6},{8,9},{9,8},{10,11... | collective-permute-start | bytes 2555912 | tf_op jit(solution)/shard_map/ppermute | solution.py:285
  280.8 2.0 collective-permute-done.6.other_ref
  282.8 1.7 shard_map.105
  (1 shorter events, 0.0 us)
Async XLA Ops:
  0.6 15.9 %copy-start.1 = (bf16[4096,128]{1,0:T(8,128)(2,1)S(1)}, bf16[4096,128]{1,0:T(8,128)(2,1)}, u32[]{:S(2)}) copy-start(bf16[4096,128]{1,0:T(8,128)(2,1)} %mine_ref.2) | copy-start | bytes 3145732
  2.3 5.3 %collective-permute-start.3 = (bf16[320,128]{1,0:T(8,128)(2,1)S(1)}, bf16[320,128]{1,0:T(8,128)(2,1)S(1)}, u32[]{:S(2)}, u32[]{:S(2)}) collective-permute-start(bf16[320,128]{1,0:T(8,128)(2,1)S(1)} %maximum_maximum_fusion.refs_0_), channel_id=1, source_target_pairs={{0,192},{64,0},{128,64},{192,128},{1,193},{65,1},{129,65},{193,129... | collective-permute-start | bytes 245768 | tf_op jit(solution)/shard_map/ppermute | solution.py:288
  5.6 4.9 %collective-permute-start.2 = (bf16[320,128]{1,0:T(8,128)(2,1)S(1)}, bf16[320,128]{1,0:T(8,128)(2,1)S(1)}, u32[]{:S(2)}, u32[]{:S(2)}) collective-permute-start(bf16[320,128]{1,0:T(8,128)(2,1)S(1)} %maximum_maximum_fusion.refs_0_), channel_id=1, source_target_pairs={{0,128},{64,192},{128,0},{192,64},{1,129},{65,193},{129,1},{193,65... | collective-permute-start | bytes 245768 | tf_op jit(solution)/shard_map/ppermute | solution.py:288
  6.2 6.4 %collective-permute-start.1 = (bf16[320,128]{1,0:T(8,128)(2,1)S(1)}, bf16[320,128]{1,0:T(8,128)(2,1)S(1)}, u32[]{:S(2)}, u32[]{:S(2)}) collective-permute-start(bf16[320,128]{1,0:T(8,128)(2,1)S(1)} %maximum_maximum_fusion.refs_0_), channel_id=1, source_target_pairs={{0,64},{64,128},{128,192},{192,0},{1,65},{65,129},{129,193},{193,1... | collective-permute-start | bytes 245768 | tf_op jit(solution)/shard_map/ppermute | solution.py:288
  12.6 4.7 %collective-permute-start.4 = (bf16[4,320,128]{2,1,0:T(8,128)(2,1)S(1)}, bf16[4,320,128]{2,1,0:T(8,128)(2,1)S(1)}, u32[]{:S(2)}, u32[]{:S(2)}) collective-permute-start(bf16[4,320,128]{2,1,0:T(8,128)(2,1)S(1)} %pad_maximum_fusion), channel_id=1, source_target_pairs={{0,1},{1,0},{2,3},{3,2},{4,5},{5,4},{6,7},{7,6},{8,9},{9,8},{10,11... | collective-permute-start | bytes 983048 | tf_op jit(solution)/shard_map/ppermute | solution.py:285
  14.8 1.7 collective-permute-start
  15.8 4.3 %collective-permute-start.5 = (bf16[512,128]{1,0:T(8,128)(2,1)S(1)}, bf16[512,128]{1,0:T(8,128)(2,1)S(1)}, u32[]{:S(2)}, u32[]{:S(2)}) collective-permute-start(bf16[512,128]{1,0:T(8,128)(2,1)S(1)} %constant_dynamic-slice_fusion), channel_id=1, source_target_pairs={{0,1},{1,0},{2,3},{3,2},{4,5},{5,4},{6,7},{7,6},{8,9},{9,8},{10,11... | collective-permute-start | bytes 393224 | tf_op jit(solution)/shard_map/ppermute | solution.py:285
  73.8 43.5 %copy-start = (bf16[4096,128]{1,0:T(8,128)(2,1)S(1)}, bf16[4096,128]{1,0:T(8,128)(2,1)}, u32[]{:S(2)}) copy-start(bf16[4096,128]{1,0:T(8,128)(2,1)} %mine_ref.3) | copy-start | bytes 3145732
  261.6 21.2 %collective-permute-start.6 = (bf16[4,832,128]{2,1,0:T(8,128)(2,1)S(1)}, bf16[4,832,128]{2,1,0:T(8,128)(2,1)S(1)}, u32[]{:S(2)}, u32[]{:S(2)}) collective-permute-start(bf16[4,832,128]{2,1,0:T(8,128)(2,1)S(1)} %shard_map.104), channel_id=1, source_target_pairs={{0,1},{1,0},{2,3},{3,2},{4,5},{5,4},{6,7},{7,6},{8,9},{9,8},{10,11... | collective-permute-start | bytes 2555912 | tf_op jit(solution)/shard_map/ppermute | solution.py:285
